TPU v7x, 128 devices: a whole 4x4x4 slice. The times are simulated.
128 devices in a mesh: wide: 16 (over z, x), narrow: 8 (over y, core).
Axes of the slice: x: 4, y: 4, z: 4, core: 2. Of those that a mesh axis runs over, the one named last changes fastest.
Arguments:
- positions: float32 [3, 6291456], P(None, ('wide', 'narrow')), may hold values from -6 to 6
- velocities: float32 [3, 6291456], P(None, ('wide', 'narrow')), may hold values from -6 to 6
- nodal_mass: float32 [6291456], P(('wide', 'narrow')), may hold values from 0.5 to 2
- thickness: float32 [6291456], P(('wide', 'narrow')), may hold values from 0.05 to 0.3
- pack_index: int32 [128, 65536], P(('wide', 'narrow')), may hold values from 0 to 49152, as said below
- connectivity: int32 [262144, 4], P(('wide', 'narrow')), may hold values from 0 to 65535, as said below
- tile_list: int32 [2, 131072], P(None, ('wide', 'narrow')), may hold values from 0 to 511, as said below
- pair_mask: int32 [131072, 256], P(('wide', 'narrow')), may hold values 0 or 1
- tile_count: int32 [128], P(('wide', 'narrow')), may hold values from 256 to 1024
Outputs:
- contact_force: float32 [3, 6291456], P(None, ('wide', 'narrow'))
Inputs may be any that keep to these rules, and one draw needn't show every extreme that they name: `pack_index`: row s lists, for each send slot p * 512 + k of mesh owner s (bound for partition p), the local node it carries, or 49152 for an empty slot. Each of the 49152 local nodes appears exactly once in its row; every block of 512 slots carries at least 128 nodes, and in every row one block is full. `connectivity`: rows p * 2048 to (p + 1) * 2048 - 1 are partition p's segments; each entry is a non-empty slot of contact_state[p], and the 8192 entries of one partition are distinct. `tile_list`: row 0 holds node blocks below 512, row 1 segment blocks below 24. Within one partition's 1024 entries the first 512 node blocks are distinct and entry t + 512 has the node block of entry t.
All inputs are finite; a program needn't handle non-finite values. No bound on the sum of `pair_mask` on one device may be relied on, other than what follows from the above.
Results may differ from a plain program's by a relative error of at most 0.0003.
Values sent between devices are 32-bit elements; how exact they have to be, the bound alone decides.
A program may use at most 128 MiB of HBM per device.

v0:
```python
import jax
import jax.numpy as jnp
from jax import lax
from jax.sharding import PartitionSpec as P

stiffness = 1.0
damping = 0.3
tiles_per_turn = 32


def padded(cells, sides, width):
    for axis, dim in sides:
        count = lax.axis_size(axis)
        ends = count - 1
        head = lax.slice_in_dim(cells, 0, width, axis=dim)
        tail = lax.slice_in_dim(cells, cells.shape[dim] - width, cells.shape[dim], axis=dim)
        cells = jnp.concatenate(
            [
                lax.ppermute(tail, axis, [(i, (i + 1) % count) for i in range(ends)]),
                cells,
                lax.ppermute(head, axis, [((i + 1) % count, i) for i in range(ends)]),
            ],
            axis=dim,
        )
    return cells


def quad_features(quad_nodes):
    corner = quad_nodes[:, 0:3]
    motion = quad_nodes[:, 3:6]
    centre = (corner[0] + corner[1] + corner[2] + corner[3]) * 0.25
    diag_one = corner[2] - corner[0]
    diag_two = corner[3] - corner[1]
    cross_raw = jnp.stack(
        [
            diag_one[1] * diag_two[2] - diag_one[2] * diag_two[1],
            diag_one[2] * diag_two[0] - diag_one[0] * diag_two[2],
            diag_one[0] * diag_two[1] - diag_one[1] * diag_two[0],
        ]
    )
    length = jnp.sqrt(jnp.sum(cross_raw * cross_raw, axis=0))
    normal = cross_raw / jnp.maximum(length, 1.0)
    drift = (motion[0] + motion[1] + motion[2] + motion[3]) * 0.25
    spread = jnp.sum((corner - centre[None]) ** 2, axis=(0, 1)) * 0.25
    return jnp.concatenate([centre, normal, drift, spread[None]], axis=0)


def neighbour_cells(ghost_rim):
    flat = ghost_rim.reshape((9,) + ghost_rim.shape[2:])
    return jnp.take(flat, jnp.array([0, 1, 2, 3, 5, 6, 7, 8], dtype=jnp.int32), axis=0)


def pair_forces(node_tile, seg_tile, mask_tile):
    position = node_tile[:, 0:3, :, None]
    centre = seg_tile[:, 0:3, None, :]
    normal = seg_tile[:, 3:6, None, :]
    signed_gap = (
        jnp.sum(position * normal, axis=1)
        - jnp.sum(centre * normal, axis=1)
        - node_tile[:, 7, :, None]
    )
    intersection = jnp.maximum(-signed_gap, 0.0)
    distance = jnp.sum((position - centre) ** 2, axis=1)
    weight = jnp.exp(-distance / (seg_tile[:, 9, None, :] + 0.25)) * mask_tile[:, None, :]
    closing = jnp.sum((node_tile[:, 3:6, :, None] - seg_tile[:, 6:9, None, :]) * normal, axis=1)
    magnitude = intersection * weight * (stiffness * node_tile[:, 6, :, None] - damping * closing)
    return jnp.sum(magnitude[:, None] * normal, axis=3)


def contact_pass(arrived, seg_all, tile_rows, mask_rows, tile_total):
    block_count = arrived.shape[1] // 128
    node_blocks = jnp.transpose(arrived.reshape(arrived.shape[0], block_count, 128), (1, 0, 2))
    seg_blocks = jnp.transpose(
        seg_all.reshape(seg_all.shape[0], seg_all.shape[1] // 256, 256), (1, 0, 2)
    )
    turns = (tile_total + tiles_per_turn - 1) // tiles_per_turn

    def one_turn(turn_index, totals):
        first_tile = (turn_index * tiles_per_turn).astype(jnp.int32)
        chosen = lax.dynamic_slice_in_dim(tile_rows, first_tile, tiles_per_turn, 1)
        mask_tile = lax.dynamic_slice_in_dim(mask_rows, first_tile, tiles_per_turn, 0).astype(
            jnp.float32
        )
        node_tile = jnp.take(node_blocks, chosen[0], axis=0)
        seg_tile = jnp.take(seg_blocks, chosen[1], axis=0)
        live_tiles = (first_tile + jnp.arange(tiles_per_turn, dtype=jnp.int32) < tile_total).astype(
            jnp.float32
        )
        tile_force = pair_forces(node_tile, seg_tile, mask_tile) * live_tiles[:, None, None]
        return totals.at[chosen[0]].add(tile_force)

    totals = lax.fori_loop(0, turns, one_turn, jnp.zeros((block_count, 3, 128), jnp.float32))
    return jnp.transpose(totals, (1, 0, 2)).reshape(3, -1)


def on_device(
    positions,
    velocities,
    nodal_mass,
    thickness,
    pack_index,
    connectivity,
    tile_list,
    pair_mask,
    tile_count,
):
    node_data = jnp.concatenate([positions, velocities, nodal_mass[None], thickness[None]], axis=0)
    slots_row = pack_index[0]
    outgoing = jnp.take(node_data, slots_row, axis=1, mode="fill", fill_value=0.0)
    arrived = lax.all_to_all(outgoing, ("wide", "narrow"), split_axis=1, concat_axis=1, tiled=True)
    quad_nodes = jnp.transpose(jnp.take(arrived[0:6], connectivity, axis=1), (2, 0, 1))
    ghost_count = connectivity.shape[0] // 4
    features = quad_features(quad_nodes)
    raw_quads = quad_nodes[:, :, :ghost_count].reshape(24, ghost_count)
    ghost_rim = padded(raw_quads[None, None], (("wide", 0), ("narrow", 1)), 1)
    cells = neighbour_cells(ghost_rim).reshape(8, 4, 6, ghost_count)
    ghost = quad_features(jnp.transpose(cells, (1, 2, 0, 3)).reshape(4, 6, 8 * ghost_count))
    seg_all = jnp.concatenate([features, ghost], axis=1)
    slot_force = contact_pass(arrived, seg_all, tile_list, pair_mask, tile_count[0])
    returned = lax.all_to_all(
        slot_force, ("wide", "narrow"), split_axis=1, concat_axis=1, tiled=True
    )
    slot_numbers = jnp.arange(slots_row.shape[0], dtype=jnp.int32)
    slot_of_node = (
        jnp.zeros((positions.shape[1],), jnp.int32).at[slots_row].set(slot_numbers, mode="drop")
    )
    return jnp.take(returned, slot_of_node, axis=1)


def solution(mesh):
    return jax.shard_map(
        on_device,
        mesh=mesh,
        in_specs=(
            P(None, ("wide", "narrow")),
            P(None, ("wide", "narrow")),
            P(("wide", "narrow")),
            P(("wide", "narrow")),
            P(("wide", "narrow"), None),
            P(("wide", "narrow"), None),
            P(None, ("wide", "narrow")),
            P(("wide", "narrow"), None),
            P(("wide", "narrow")),
        ),
        out_specs=P(None, ("wide", "narrow")),
        check_vma=False,
    )
```

profile of v0, /device:TPU:1, one launch (start us, length us, event | category | flops | bytes accessed | tf_op | source)
XLA Modules:
  0.0 1458.3 jit_solution(9895597628669673153)
XLA Ops:
  3.6 12.9 copy.77
  16.5 223.7 %gather_fusion.2 = f32[65536,8]{1,0:T(8,128)} fusion(f32[8,49152]{0,1:T(8,128)} %copy.77, s32[65536]{0:T(1024)S(1)} %broadcast_clamp_fusion), kind=kCustom, calls=%fused_computation.2 | custom fusion | bytes 4456448 | tf_op jit(solution)/shard_map/jit(_take)/gather | solution.py:109
  240.2 17.7 %copy.78 = f32[8,128,512]{2,0,1:T(8,128)S(1)} copy(f32[8,128,512]{0,2,1:T(8,128)} %bitcast.138) | data formatting | bytes 4194304 | tf_op jit(solution)/shard_map/jit(_take)/gather | solution.py:109
  261.5 11.5 all-to-all-start
  274.8 239.7 %scatter_custom_fusion.1 = s32[49152]{0:T(1024)S(1)} fusion(s32[65536]{0:T(1024)S(1)} %bitcast.149, s32[65536]{0:T(1024)S(1)} %iota.8, s32[]{:T(128)} %constant.101.clone.1), kind=kCustom, calls=%fused_computation.52 | custom fusion | bytes 196612 | tf_op jit(solution)/shard_map/scatter | solution.py:125
  514.6 15.6 %copy.80 = f32[6,128,512]{0,2,1:T(8,128)} copy(f32[6,128,512]{2,0,1:T(8,128)S(1)} %bitcast.140) | data formatting | bytes 3145728 | tf_op jit(solution)/shard_map/slice | solution.py:111
  530.2 38.2 %gather_fusion.3 = f32[8192,6]{1,0:T(8,128)} fusion(f32[6,65536]{0,1:T(8,128)} %bitcast.136, s32[8192]{0:T(1024)S(1)} %broadcast_clamp_fusion.1), kind=kCustom, calls=%fused_computation.3 | custom fusion | bytes 425984 | tf_op jit(solution)/shard_map/jit(_take)/gather | solution.py:111
  583.7 3.7 collective-permute-start.2
  589.5 4.3 collective-permute-done.3
  597.5 188.7 %while.10 = (s32[]{:T(128)}, f32[512,3,128]{2,1,0:T(4,128)}, s32[]{:T(128)}, s32[2,1024]{1,0:T(2,128)}, f32[512,8,128]{2,1,0:T(8,128)}, /*index=5*/f32[24,10,256...) while((s32[]{:T(128)}, f32[512,3,128]{2,1,0:T(4,128)}, ...), condition=%wide.region_12.13_spmd, body=%wide.region_5.0_spmd.sunk | while | flops 40032932 | bytes 37398960 | solution.py:92
  601.4 5.4 multiply_reduce_fusion.11
  620.2 5.4 multiply_reduce_fusion.11
  631.5 3.7 scatter_fusion
  639.1 5.4 multiply_reduce_fusion.11
  650.4 3.7 scatter_fusion
  658.0 5.4 multiply_reduce_fusion.11
  676.9 5.4 multiply_reduce_fusion.11
  688.1 3.7 scatter_fusion
  695.7 5.4 multiply_reduce_fusion.11
  707.0 3.7 scatter_fusion
  714.6 5.4 multiply_reduce_fusion.11
  725.9 3.7 scatter_fusion
  733.5 5.4 multiply_reduce_fusion.11
  752.4 5.4 multiply_reduce_fusion.11
  763.6 3.7 scatter_fusion
  771.2 5.4 multiply_reduce_fusion.11
  786.2 423.8 %all-to-all-start.1 = ((f32[3,128,512]{2,0,1:T(4,128)}), f32[3,128,512]{2,0,1:T(4,128)S(1)}, u32[]{:S(2)}, u32[]{:S(2)}) async-start(f32[3,128,512]{2,0,1:T(4,128)} %bitcast.38), calls=%async_computation.1 | async-start | bytes 2097152 | tf_op jit(solution)/shard_map/all_to_all | solution.py:120
  1210.0 18.7 %all-to-all-done.1 = f32[3,128,512]{2,0,1:T(4,128)S(1)} async-done(((f32[3,128,512]{2,0,1:T(4,128)}), f32[3,128,512]{2,0,1:T(4,128)S(1)}, u32[]{:S(2)}, u32[]{:S(2)}) %all-to-all-start.1) | async-done | bytes 786464 | tf_op jit(solution)/shard_map/all_to_all | solution.py:120
  1228.8 15.6 %copy.94 = f32[3,128,512]{0,2,1:T(8,128)} copy(f32[3,128,512]{2,0,1:T(4,128)S(1)} %all-to-all-done.1) | data formatting | bytes 1572864 | tf_op jit(solution)/shard_map/all_to_all | solution.py:120
  1244.4 172.4 %gather_fusion.5 = f32[49152,3]{1,0:T(8,128)} fusion(f32[3,65536]{0,1:T(8,128)} %bitcast.137, s32[49152]{0:T(1024)S(1)} %fusion.4), kind=kCustom, calls=%fused_computation.5 | custom fusion | bytes 1376256 | tf_op jit(solution)/shard_map/jit(_take)/gather | solution.py:127
  1416.8 27.4 %select_bitcast_fusion = f32[3,49152]{0,1:T(8,128)} fusion(f32[49152,3]{1,0:T(8,128)} %gather_fusion.5, pred[49152]{0:T(1024)(128)(4,1)S(1)} %compare_and_fusion.3), kind=kLoop, calls=%fused_computation.32 | loop fusion | flops 147456 | bytes 1228800 | tf_op jit(solution)/shard_map/jit(_take)/select_n | solution.py:127
  1444.2 14.1 copy.95
  (251 shorter events, 140.6 us)
Async XLA Ops:
  240.2 18.3 %copy-start = (s32[1,65536]{1,0:T(1,128)S(1)}, s32[1,65536]{1,0:T(1,128)}, u32[]{:S(2)}) copy-start(s32[1,65536]{1,0:T(1,128)} %param.16) | copy-start | bytes 786436
  259.8 13.2 copy-start.1
  259.8 13.2 copy-start.2
  261.5 253.1 %all-to-all-start = ((f32[8,128,512]{2,0,1:T(8,128)}), f32[8,128,512]{2,0,1:T(8,128)S(1)}, u32[]{:S(2)}, u32[]{:S(2)}) async-start(f32[8,128,512]{2,0,1:T(8,128)} %broadcast_select_fusion.2), calls=%async_computation | async-start | bytes 4194304 | tf_op jit(solution)/shard_map/all_to_all | solution.py:110
  572.1 11.6 collective-permute-start
  575.3 8.4 collective-permute-start.1
  583.7 5.8 collective-permute-start.2
  587.4 6.5 collective-permute-start.3
  786.2 442.6 %all-to-all-start.1 = ((f32[3,128,512]{2,0,1:T(4,128)}), f32[3,128,512]{2,0,1:T(4,128)S(1)}, u32[]{:S(2)}, u32[]{:S(2)}) async-start(f32[3,128,512]{2,0,1:T(4,128)} %bitcast.38), calls=%async_computation.1 | async-start | bytes 2097152 | tf_op jit(solution)/shard_map/all_to_all | solution.py:120
where the time goes:
time: 1460 us
  local copies, waits for them, and re-layouts  800 us (55%)
  starting transfers between devices  446 us (31%)
  other arithmetic  187 us (13%)
  waiting for transfers between devices  23.1 us (2%)
    all_to_all x1, starting transfers between devices, on_device(): lax.all_to_all(slot_force, ('wide', 'narrow'), split_axis=1, concat_axis=...  424 us
    gather x2, local copies, waits for them, and re-layouts, on_device(): jnp.take(node_data, slots_row, axis=1, mode='fill', fill_value=0.0)  241 us
    scatter x1, local copies, waits for them, and re-layouts, on_device(): jnp.zeros((positions.shape[1],), jnp.int32).at[slots_row]  240 us
    gather x1, local copies, waits for them, and re-layouts, on_device(): return jnp.take(returned, slot_of_node, axis=1)  172 us
    reduce_sum x10, other arithmetic, pair_forces(): jnp.sum(position * normal, axis=1) - jnp.sum(centre * normal, axis=1)  54 us
    gather x2, local copies, waits for them, and re-layouts, on_device(): jnp.take(arrived[0:6], connectivity, axis=1)  41.8 us
    scatter-add x10, other arithmetic, one_turn(): return totals.at[chosen[0]].add(tile_force)  36.5 us
  transfers between devices with their start and end apart: 6, of which 2 were waited for; matrix products, arithmetic and copies ran while one was open for 17% of the time, Pallas kernels for 0%

commit v1 on v0

v1 whole, which is shorter than its diff:
```python
import functools
import jax
import jax.numpy as jnp
from jax import lax
from jax.experimental import pallas as pl
from jax.experimental.pallas import tpu as pltpu
from jax.sharding import PartitionSpec as P

F32 = jnp.float32
BF16 = jnp.bfloat16
I32 = jnp.int32
CHUNK = 256
LOG2E = 1.4426950408889634


def iota(shape, axis):
    return lax.broadcasted_iota(I32, shape, axis)


def split3(x):
    high = x.astype(BF16)
    rest = x - high.astype(F32)
    middle = rest.astype(BF16)
    low = (rest - middle.astype(F32)).astype(BF16)
    return high, middle, low


def expand_rows(tile):
    rows = tile.shape[0]
    high, middle, low = split3(tile)
    parts = [high.astype(F32), middle.astype(F32), low.astype(F32)]
    stacked = jnp.concatenate(parts, axis=0).astype(BF16)
    spread = (iota((3 * rows, 128), 0) % rows == iota((3 * rows, 128), 1) % 8).astype(F32).astype(BF16)
    return lax.dot_general(stacked, spread, (((0,), (0,)), ((), ())), preferred_element_type=F32)


def merge_groups(rows, shape):
    lane = iota(shape, 1)
    bit = 8
    while len(rows) > 1:
        odd = (lane & bit) != 0
        rows = [jnp.where(odd, rows[2 * i + 1], rows[2 * i]) for i in range(len(rows) // 2)]
        bit *= 2
    return rows[0]


def feature_major(rows):
    lane = iota((8, 128), 1)
    pick = (lane // 8) * 8 + iota((8, 128), 0)
    out = None
    for r in range(8):
        moved = jnp.take_along_axis(rows[r], pick, axis=1)
        out = moved if out is None else jnp.where(lane % 8 == r, moved, out)
    return out


def index_chunks(index_ref, body):
    def turn(i, carry):
        body(i, lambda k: index_ref[0, i * CHUNK + k])
        return carry

    lax.fori_loop(0, index_ref.shape[1] // CHUNK, turn, 0, unroll=2)


def pack_kernel(index_ref, pos_ref, vel_ref, mass_ref, thick_ref, out_ref, rows_ref):
    nodes = pos_ref.shape[1]

    def fill(b, carry):
        at = pl.ds(pl.multiple_of(b * 128, 128), 128)
        tile = jnp.concatenate([pos_ref[:, at], vel_ref[:, at], mass_ref[:, at], thick_ref[:, at]], axis=0)
        rows_ref[at, :] = expand_rows(tile)
        return carry

    lax.fori_loop(0, nodes // 128, fill, 0, unroll=8)
    rows_ref[nodes : nodes + 8, :] = jnp.zeros((8, 128), F32)

    def chunk(c, index):
        for half in range(CHUNK // 128):
            lines = []
            for r in range(8):
                got = [
                    rows_ref[pl.ds(index(half * 128 + k * 8 + r), 8, stride=0), :] for k in range(16)
                ]
                lines.append(merge_groups(got, (8, 128)))
            out_ref[c * (CHUNK // 128) + half] = feature_major(lines)

    index_chunks(index_ref, chunk)


VMEM = pl.BlockSpec(memory_space=pltpu.VMEM)
SMEM = pl.BlockSpec(memory_space=pltpu.SMEM)


def pack(positions, velocities, nodal_mass, thickness, pack_index):
    nodes = positions.shape[1]
    return pl.pallas_call(
        pack_kernel,
        out_shape=jax.ShapeDtypeStruct((pack_index.shape[1] // 128, 8, 128), F32),
        in_specs=[SMEM, VMEM, VMEM, VMEM, VMEM],
        out_specs=VMEM,
        scratch_shapes=[
            pltpu.VMEM((nodes + 8, 128), F32),
        ],
        compiler_params=pltpu.CompilerParams(vmem_limit_bytes=48 << 20),
        name="pack",
    )(pack_index, positions, velocities, nodal_mass.reshape(1, -1), thickness.reshape(1, -1))


def scatter_kernel(index_ref, force_ref, out_ref, rows_ref, ex_a, ex_b):
    nodes = out_ref.shape[1]

    def chunk(c, index):
        for half, ex in enumerate((ex_a, ex_b)):
            ex[...] = expand_rows(force_ref[c * 2 + half])
            for j in range(128):
                rows_ref[pl.ds(index(half * 128 + j), 1), :] = ex[j : j + 1, :]

    index_chunks(index_ref, chunk)

    def collect(b, carry):
        at = pl.multiple_of(b * 128, 128)
        tiles = [rows_ref[pl.ds(at + k * 8, 8), :] for k in range(16)]
        merged = merge_groups(tiles, (8, 128))
        lines = [jnp.broadcast_to(merged[r : r + 1], (8, 128)) for r in range(8)]
        out_ref[:, pl.ds(at, 128)] = feature_major(lines)[0:3]
        return carry

    lax.fori_loop(0, nodes // 128, collect, 0, unroll=4)


def scatter(force, pack_index, nodes):
    return pl.pallas_call(
        scatter_kernel,
        out_shape=jax.ShapeDtypeStruct((3, nodes), F32),
        in_specs=[SMEM, VMEM],
        out_specs=VMEM,
        scratch_shapes=[
            pltpu.VMEM((nodes + 8, 128), F32),
            pltpu.VMEM((128, 128), F32),
            pltpu.VMEM((128, 128), F32),
        ],
        compiler_params=pltpu.CompilerParams(vmem_limit_bytes=48 << 20),
        name="scatter",
    )(pack_index, force)


def features_kernel(conn_ref, state_ref, out_ref):
    lane = iota((8, 128), 1)

    def chunk(c, carry):
        corner = []
        for i in range(4):
            found = jnp.zeros((8, 128), F32)
            for q in range(128):
                slot = conn_ref[i, c * 128 + q]
                tile = state_ref[slot >> 7]
                moved = pltpu.roll(tile, (q - slot) & 127, axis=1)
                found = jnp.where(lane == q, moved, found)
            corner.append(found)
        total = (corner[0] + corner[1] + corner[2] + corner[3]) * 0.25
        centre = total[0:3]
        d1 = corner[2] - corner[0]
        d2 = corner[3] - corner[1]
        w0 = d1[1:2] * d2[2:3] - d1[2:3] * d2[1:2]
        w1 = d1[2:3] * d2[0:1] - d1[0:1] * d2[2:3]
        w2 = d1[0:1] * d2[1:2] - d1[1:2] * d2[0:1]
        scale = jnp.maximum(jnp.sqrt(w0 * w0 + w1 * w1 + w2 * w2), 1.0)
        off = [corner[i][0:3] - centre for i in range(4)]
        square = off[0] * off[0] + off[1] * off[1] + off[2] * off[2] + off[3] * off[3]
        spread = (square[0:1] + square[1:2] + square[2:3]) * 0.25
        at = pl.ds(pl.multiple_of(c * 128, 128), 128)
        out_ref[0:3, at] = centre
        out_ref[3:6, at] = jnp.concatenate([w0 / scale, w1 / scale, w2 / scale], axis=0)
        out_ref[6:9, at] = total[3:6]
        out_ref[9:10, at] = spread
        return carry

    lax.fori_loop(0, out_ref.shape[1] // 128, chunk, 0)


def features(connectivity, state):
    segs = connectivity.shape[0]
    return pl.pallas_call(
        features_kernel,
        out_shape=jax.ShapeDtypeStruct((10, segs), F32),
        in_specs=[SMEM, VMEM],
        out_specs=VMEM,
        compiler_params=pltpu.CompilerParams(vmem_limit_bytes=16 << 20),
        name="features",
    )(connectivity.T, state)


def contact_kernel(tiles_ref, count_ref, state_ref, seg_ref, mask_ref, out_ref, coef_ref, normal_ref, *, stiffness, damping):
    blocks = state_ref.shape[0]
    seg_blocks = seg_ref.shape[1] // 256
    out_ref[...] = jnp.zeros_like(out_ref)

    def stack_seg(rows):
        zero = jnp.zeros((1, 256), F32)
        block = jnp.concatenate([zero if r is None else r for r in rows] + [zero] * (16 - len(rows)), axis=0)
        high, middle, low = split3(block)
        return jnp.concatenate([high, high, high, middle, middle, low], axis=0)

    def prepare(s, carry):
        f = seg_ref[:, pl.ds(pl.multiple_of(s * 256, 256), 256)]
        c = [f[i : i + 1] for i in range(3)]
        n = [f[i : i + 1] for i in range(3, 6)]
        u = [f[i : i + 1] for i in range(6, 9)]
        rate = LOG2E / (f[9:10] + 0.25)
        one = jnp.ones((1, 256), F32)
        dot = lambda a, b: a[0] * b[0] + a[1] * b[1] + a[2] * b[2]
        depth = [-n[0], -n[1], -n[2], None, None, None, None, one, None, dot(c, n)]
        power = [2.0 * rate * c[0], 2.0 * rate * c[1], 2.0 * rate * c[2], None, None, None, None, None, -rate, -rate * dot(c, c)]
        push = [None, None, None, -damping * n[0], -damping * n[1], -damping * n[2], stiffness * one, None, None, damping * dot(u, n)]
        coef_ref[s, 0] = stack_seg(depth)
        coef_ref[s, 1] = stack_seg(power)
        coef_ref[s, 2] = stack_seg(push)
        high, middle, _ = split3(f[3:6])
        normal_ref[s] = jnp.concatenate([high.astype(F32), middle.astype(F32), jnp.zeros((2, 256), F32)], axis=0)
        return carry

    lax.fori_loop(0, seg_blocks, prepare, 0)
    total = count_ref[0]
    row = iota((8, 128), 0)

    def tile_pair(t, carry):
        block = tiles_ref[0, t]
        node = state_ref[block]
        sq = jnp.sum(jnp.where(row < 3, node * node, 0.0), axis=0, keepdims=True)
        extra = jnp.where(row == 0, sq, jnp.where(row == 1, 1.0, 0.0))
        high, middle, low = split3(jnp.concatenate([node, extra], axis=0))
        nodes = jnp.concatenate([high, middle, low, high, middle, high], axis=0).T
        force = jnp.zeros((8, 128), F32)
        for half in range(2):
            e = t + half * blocks
            s = tiles_ref[1, e]
            live = (e < total).astype(F32)
            term = [
                jnp.dot(nodes, coef_ref[s, i], preferred_element_type=F32) for i in range(3)
            ]
            size = jnp.maximum(term[0], 0.0) * jnp.exp2(term[1]) * term[2]
            top = size.astype(BF16)
            rest = (size - top.astype(F32)).astype(BF16)
            mask = mask_ref[pl.ds(e, 1), :].astype(F32) * live
            weights = (normal_ref[s] * mask).astype(BF16)
            for part in (top, rest):
                force += lax.dot_general(weights, part, (((1,), (1,)), ((), ())), preferred_element_type=F32)
        out_ref[block, 0:3] = force[0:3] + force[3:6]
        return carry

    lax.fori_loop(0, jnp.minimum(total, blocks), tile_pair, 0)


def contact(state, seg_all, tile_list, pair_mask, tile_count, stiffness, damping):
    blocks = state.shape[0]
    seg_blocks = seg_all.shape[1] // 256
    return pl.pallas_call(
        functools.partial(contact_kernel, stiffness=stiffness, damping=damping),
        out_shape=jax.ShapeDtypeStruct((blocks, 4, 128), F32),
        in_specs=[SMEM, SMEM, VMEM, VMEM, VMEM],
        out_specs=VMEM,
        scratch_shapes=[
            pltpu.VMEM((seg_blocks, 3, 96, 256), BF16),
            pltpu.VMEM((seg_blocks, 8, 256), F32),
        ],
        compiler_params=pltpu.CompilerParams(vmem_limit_bytes=32 << 20),
        name="contact",
    )(tile_list, tile_count, state, seg_all, pair_mask)


STIFFNESS = 1.0
DAMPING = 0.3
AXES = ("wide", "narrow")


def swap(blocks):
    return lax.all_to_all(blocks, AXES, split_axis=0, concat_axis=0, tiled=True)


def padded(cells, sides):
    for axis, dim in sides:
        ends = lax.axis_size(axis) - 1
        head = lax.slice_in_dim(cells, 0, 1, axis=dim)
        tail = lax.slice_in_dim(cells, cells.shape[dim] - 1, cells.shape[dim], axis=dim)
        before = lax.ppermute(tail, axis, [(i, i + 1) for i in range(ends)])
        after = lax.ppermute(head, axis, [(i + 1, i) for i in range(ends)])
        cells = jnp.concatenate([before, cells, after], axis=dim)
    return cells


def on_device(positions, velocities, nodal_mass, thickness, pack_index, connectivity, tile_list, pair_mask, tile_count):
    state = swap(pack(positions, velocities, nodal_mass, thickness, pack_index))
    own = features(connectivity, state)
    ghosts = connectivity.shape[0] // 4
    rim = padded(own[None, None, :, :ghosts], (("wide", 0), ("narrow", 1)))
    around = [rim[i, j] for i in range(3) for j in range(3) if (i, j) != (1, 1)]
    seg_all = jnp.concatenate([own] + around, axis=1)
    force = contact(state, seg_all, tile_list, pair_mask, tile_count, STIFFNESS, DAMPING)
    return scatter(swap(force), pack_index, positions.shape[1])


def solution(mesh):
    return jax.shard_map(
        on_device,
        mesh=mesh,
        in_specs=(
            P(None, AXES),
            P(None, AXES),
            P(AXES),
            P(AXES),
            P(AXES, None),
            P(AXES, None),
            P(None, AXES),
            P(AXES, None),
            P(AXES),
        ),
        out_specs=P(None, AXES),
        check_vma=False,
    )
```

time: 1460 us -> 597 us (0.41)
  local copies, waits for them, and re-layouts: 800 us -> 5.13 us
  starting transfers between devices: 446 us -> 9.48 us
  Pallas kernels: 0 us -> 357 us
  blocking collectives: 0 us -> 217 us
  other arithmetic: 187 us -> 0.01 us
  waiting for transfers between devices: 23.1 us -> 5.93 us
    gather x27 -> x0, local copies, waits for them, and re-layouts: 484 us -> none  [the longest x2 241 us: on_device(): jnp.take(node_data, slots_row, axis=1, mode='fill', fill_value=0.0)]
    all_to_all x2 -> x0, starting transfers between devices: 435 us -> none  [the longest x1 424 us: on_device(): lax.all_to_all(slot_force, ('wide', 'narrow'), split_axis=1, concat_axis=...]
    pallas_call x0 -> x4, Pallas kernels: none -> 357 us  [the longest x1 154 us: contact(): pl.pallas_call(functools.partial(contact_kernel, stiffness=stiffness, dam...]
    scatter x1 -> x0, local copies, waits for them, and re-layouts: 240 us -> none  [on_device(): jnp.zeros((positions.shape[1],), jnp.int32).at[slots_row]]
    all_to_all x0 -> x2, blocking collectives: none -> 217 us  [swap(): return lax.all_to_all(blocks, AXES, split_axis=0, concat_axis=0, tiled=True)]
    reduce_sum x34 -> x0, other arithmetic: 74.1 us -> none  [the longest x10 54 us: pair_forces(): jnp.sum(position * normal, axis=1) - jnp.sum(centre * normal, axis=1)]
    scatter-add x10 -> x0, other arithmetic: 36.5 us -> none  [one_turn(): return totals.at[chosen[0]].add(tile_force)]
    select_n x35 -> x0, other arithmetic: 32.4 us -> none  [the longest x1 27.4 us: on_device(): return jnp.take(returned, slot_of_node, axis=1)]
  transfers between devices with their start and end apart: 6 -> 4, of which waited for: 2 -> 2; matrix products, arithmetic and copies ran while one was open for 17% -> 0% of each run, Pallas kernels for 0% -> 0%
where the time goes in v1:
time: 597 us; the launch traced here: 595 us
  Pallas kernels  357 us (60%)
  blocking collectives  217 us (36%)
  starting transfers between devices  9.48 us (2%)
    all_to_all x2, blocking collectives, swap(): return lax.all_to_all(blocks, AXES, split_axis=0, concat_axis=0, tiled=True)  217 us
    pallas_call x1, Pallas kernels, contact(): pl.pallas_call(functools.partial(contact_kernel, stiffness=stiffness, dam...  154 us
    pallas_call x1, Pallas kernels, scatter(): pl.pallas_call(scatter_kernel, out_shape=jax.ShapeDtypeStruct((3, nodes),...  97.9 us
    pallas_call x1, Pallas kernels, pack(): pl.pallas_call(pack_kernel, out_shape=jax.ShapeDtypeStruct((pack_index.sh...  78.5 us
    pallas_call x1, Pallas kernels, features(): pl.pallas_call(features_kernel, out_shape=jax.ShapeDtypeStruct((10, segs)...  25.8 us
  transfers between devices with their start and end apart: 4, of which 2 were waited for; matrix products, arithmetic and copies ran while one was open for 0% of the time, Pallas kernels for 0%

profile of v1, /device:TPU:1, one launch (start us, length us, event | category | flops | bytes accessed | tf_op | source)
XLA Modules:
  0.0 595.1 jit_solution(963396667636177305)
XLA Ops:
  0.0 0.0 copy-start.1
  0.0 0.9 copy-done.1
  1.0 0.0 copy-start.2
  1.0 1.1 copy-done.2
  2.1 0.0 copy-start.3
  2.1 1.1 copy-done.3
  3.2 0.0 copy-start.4
  3.2 0.9 copy-done.4
  4.1 0.0 copy-start.5
  4.1 0.9 copy-done.5
  5.1 78.5 %pack.1 = f32[512,8,128]{2,1,0:T(8,128)S(1)} custom-call(s32[1,65536]{1,0:T(1,128)S(1)} %copy-done.1, f32[3,49152]{1,0:T(4,128)S(1)} %copy-done.2, f32[3,49152]{1,0:T(4,128)S(1)} %copy-done.3, f32[1,49152]{1,0:T(1,128)S(1)} %bitcast.33, f32[1,49152]{1,0:T(1,128)S(1)} %bitcast.34), custom_call_target="tpu_custom_call" | custom-call | tf_op jit(solution)/shard_map/pack/pallas_call | solution.py:96
  83.6 0.0 copy-start.6
  83.6 41.4 %all_to_all.10.state_ref = f32[512,8,128]{2,1,0:T(8,128)S(1)} all-to-all(f32[512,8,128]{2,1,0:T(8,128)S(1)} %pack.1), channel_id=1, replica_groups=mesh['wide'=16,'narrow'=8] {'wide','narrow'}, dimensions={0} | all-to-all | bytes 4194304 | tf_op jit(solution)/shard_map/all_to_all | solution.py:277
  125.0 0.0 copy-start
  125.0 0.0 copy-start.7
  125.0 0.0 copy-done.6
  125.0 25.8 %features.1 = f32[10,2048]{1,0:T(8,128)S(1)} custom-call(s32[4,2048]{1,0:T(4,128)S(1)} %bitcast.35, f32[512,8,128]{2,1,0:T(8,128)S(1)} %all_to_all.10.state_ref), custom_call_target="tpu_custom_call" | custom-call | tf_op jit(solution)/shard_map/features/pallas_call | solution.py:183
  150.8 2.3 collective-permute-start
  153.1 1.3 collective-permute-start.1
  155.0 0.0 collective-permute-done
  155.0 2.7 collective-permute-done.1
  157.8 3.2 collective-permute-start.2
  161.0 2.7 collective-permute-start.3
  163.7 0.0 collective-permute-done.2
  163.7 3.2 collective-permute-done.3
  167.0 0.0 copy-done
  167.0 0.0 copy-done.7
  167.0 154.4 %contact.1 = f32[512,4,128]{2,1,0:T(4,128)S(1)} custom-call(s32[2,1024]{1,0:T(2,128)S(1)} %copy-done.7, s32[1]{0:T(128)S(6)} %copy.18.count_ref, f32[512,8,128]{2,1,0:T(8,128)S(1)} %all_to_all.10.state_ref, f32[10,6144]{1,0:T(8,128)S(1)} %fusion.seg_ref, s32[1024,256]{1,0:T(8,128)S(1)} %copy-done), custom_call_target="tpu_custom_call" | custom-call | tf_op jit(solution)/shard_map/contact/pallas_call | solution.py:257
  321.4 175.7 %all_to_all.11.force_ref = f32[512,4,128]{2,1,0:T(4,128)S(1)} all-to-all(f32[512,4,128]{2,1,0:T(4,128)S(1)} %contact.1), channel_id=1, replica_groups=mesh['wide'=16,'narrow'=8] {'wide','narrow'}, dimensions={0} | all-to-all | bytes 2097152 | tf_op jit(solution)/shard_map/all_to_all | solution.py:277
  497.1 97.9 %scatter.1 = f32[3,49152]{1,0:T(4,128)} custom-call(s32[1,65536]{1,0:T(1,128)S(1)} %copy-done.1, f32[512,4,128]{2,1,0:T(4,128)S(1)} %all_to_all.11.force_ref), custom_call_target="tpu_custom_call" | custom-call | tf_op jit(solution)/shard_map/scatter/pallas_call | solution.py:132
  (11 shorter events, 0.1 us)
Async XLA Ops:
  0.0 0.9 copy-start.1
  1.0 1.1 copy-start.2
  2.1 1.1 copy-start.3
  3.2 0.9 copy-start.4
  4.1 0.9 copy-start.5
  83.6 41.4 %copy-start.6 = (s32[2048,4]{0,1:T(4,128)S(1)}, s32[2048,4]{0,1:T(4,128)}, u32[]{:S(2)}) copy-start(s32[2048,4]{0,1:T(4,128)} %param.14) | copy-start | bytes 98308
  125.0 42.0 %copy-start = (s32[1024,256]{1,0:T(8,128)S(1)}, s32[1024,256]{1,0:T(8,128)}, u32[]{:S(2)}) copy-start(s32[1024,256]{1,0:T(8,128)} %mask_ref.1) | copy-start | bytes 3145732
  125.0 42.0 %copy-start.7 = (s32[2,1024]{1,0:T(2,128)S(1)}, s32[2,1024]{1,0:T(2,128)}, u32[]{:S(2)}) copy-start(s32[2,1024]{1,0:T(2,128)} %tiles_ref.1) | copy-start | bytes 24580
  150.8 4.3 collective-permute-start
  153.1 4.7 collective-permute-start.1
  157.8 5.9 collective-permute-start.2
  161.0 5.9 collective-permute-start.3

commit v2 on v1

--- a/solution.py
+++ b/solution.py
@@ -10,6 +10,7 @@
 BF16 = jnp.bfloat16
 I32 = jnp.int32
 CHUNK = 256
+GROUP = 4
 LOG2E = 1.4426950408889634
 
 
@@ -190,65 +191,90 @@
     )(connectivity.T, state)
 
 
-def contact_kernel(tiles_ref, count_ref, state_ref, seg_ref, mask_ref, out_ref, coef_ref, normal_ref, *, stiffness, damping):
+def contact_kernel(tiles_ref, count_ref, state_ref, seg_ref, mask_ref, out_ref, coef_ref, normal_ref, keep_a, keep_b, *, stiffness, damping):
     blocks = state_ref.shape[0]
     seg_blocks = seg_ref.shape[1] // 256
     out_ref[...] = jnp.zeros_like(out_ref)
 
-    def stack_seg(rows):
-        zero = jnp.zeros((1, 256), F32)
-        block = jnp.concatenate([zero if r is None else r for r in rows] + [zero] * (16 - len(rows)), axis=0)
-        high, middle, low = split3(block)
-        return jnp.concatenate([high, high, high, middle, middle, low], axis=0)
-
     def prepare(s, carry):
         f = seg_ref[:, pl.ds(pl.multiple_of(s * 256, 256), 256)]
-        c = [f[i : i + 1] for i in range(3)]
-        n = [f[i : i + 1] for i in range(3, 6)]
-        u = [f[i : i + 1] for i in range(6, 9)]
+        n = f[3:6]
         rate = LOG2E / (f[9:10] + 0.25)
         one = jnp.ones((1, 256), F32)
-        dot = lambda a, b: a[0] * b[0] + a[1] * b[1] + a[2] * b[2]
-        depth = [-n[0], -n[1], -n[2], None, None, None, None, one, None, dot(c, n)]
-        power = [2.0 * rate * c[0], 2.0 * rate * c[1], 2.0 * rate * c[2], None, None, None, None, None, -rate, -rate * dot(c, c)]
-        push = [None, None, None, -damping * n[0], -damping * n[1], -damping * n[2], stiffness * one, None, None, damping * dot(u, n)]
-        coef_ref[s, 0] = stack_seg(depth)
-        coef_ref[s, 1] = stack_seg(power)
-        coef_ref[s, 2] = stack_seg(push)
-        high, middle, _ = split3(f[3:6])
-        normal_ref[s] = jnp.concatenate([high.astype(F32), middle.astype(F32), jnp.zeros((2, 256), F32)], axis=0)
+        zero = jnp.zeros((3, 256), F32)
+        dot = lambda a, b: jnp.sum(a * b, axis=0, keepdims=True)
+        sides = (
+            [-n, dot(f[0:3], n), one],
+            [2.0 * rate * f[0:3], -rate * dot(f[0:3], f[0:3]), -rate],
+            [-damping * n, damping * dot(f[6:9], n), stiffness * one],
+        )
+        for i, rows in enumerate(sides):
+            high, middle, low = split3(jnp.concatenate(rows + [zero], axis=0))
+            coef_ref[s, i] = pack6([high, high, high, middle, middle, low]).T
+        high, middle, _ = split3(n)
+        normal_ref[s] = jnp.concatenate([high.astype(F32), middle.astype(F32), zero[0:2]], axis=0)
         return carry
 
     lax.fori_loop(0, seg_blocks, prepare, 0)
     total = count_ref[0]
     row = iota((8, 128), 0)
 
-    def tile_pair(t, carry):
+    def first(t, keep_ref, slot):
         block = tiles_ref[0, t]
         node = state_ref[block]
         sq = jnp.sum(jnp.where(row < 3, node * node, 0.0), axis=0, keepdims=True)
-        extra = jnp.where(row == 0, sq, jnp.where(row == 1, 1.0, 0.0))
-        high, middle, low = split3(jnp.concatenate([node, extra], axis=0))
-        nodes = jnp.concatenate([high, middle, low, high, middle, high], axis=0).T
+        one = jnp.ones((1, 128), F32)
+        zero = jnp.zeros((3, 128), F32)
+        sides = (
+            [node[0:3], one, node[7:8]],
+            [node[0:3], one, sq],
+            [node[3:6], one, node[6:7]],
+        )
+        left = []
+        for rows in sides:
+            high, middle, low = split3(jnp.concatenate(rows + [zero], axis=0))
+            left.append(pack6([high, middle, low, high, middle, high]))
+        for half in range(2):
+            s = tiles_ref[1, t + half * blocks]
+            term = [jnp.dot(coef_ref[s, i], left[i], preferred_element_type=F32) for i in range(3)]
+            size = jnp.maximum(term[0], 0.0) * jnp.exp2(term[1]) * term[2]
+            top = size.astype(BF16)
+            keep_ref[2 * slot + half, 0] = top
+            keep_ref[2 * slot + half, 1] = (size - top.astype(F32)).astype(BF16)
+
+    def second(t, keep_ref, slot, on):
         force = jnp.zeros((8, 128), F32)
         for half in range(2):
             e = t + half * blocks
-            s = tiles_ref[1, e]
-            live = (e < total).astype(F32)
-            term = [
-                jnp.dot(nodes, coef_ref[s, i], preferred_element_type=F32) for i in range(3)
-            ]
-            size = jnp.maximum(term[0], 0.0) * jnp.exp2(term[1]) * term[2]
-            top = size.astype(BF16)
-            rest = (size - top.astype(F32)).astype(BF16)
+            live = jnp.where(e < total, on, 0.0)
             mask = mask_ref[pl.ds(e, 1), :].astype(F32) * live
-            weights = (normal_ref[s] * mask).astype(BF16)
-            for part in (top, rest):
-                force += lax.dot_general(weights, part, (((1,), (1,)), ((), ())), preferred_element_type=F32)
-        out_ref[block, 0:3] = force[0:3] + force[3:6]
-        return carry
-
-    lax.fori_loop(0, jnp.minimum(total, blocks), tile_pair, 0)
+            weights = (normal_ref[tiles_ref[1, e]] * mask).astype(BF16)
+            for part in range(2):
+                force += jnp.dot(weights, keep_ref[2 * slot + half, part], preferred_element_type=F32)
+        out_ref[tiles_ref[0, t], 0:3] = force[0:3] + force[3:6]
+
+    keep_b[...] = jnp.zeros_like(keep_b)
+
+    def turn(i, carry):
+        t = i * (2 * GROUP)
+        before = jnp.maximum(t - GROUP, 0)
+        on = jnp.where(i > 0, 1.0, 0.0)
+        for k in range(GROUP):
+            first(t + k, keep_a, k)
+            second(before + k, keep_b, k, on)
+        for k in range(GROUP):
+            first(t + GROUP + k, keep_b, k)
+            second(t + k, keep_a, k, 1.0)
+        return carry
+
+    turns = (jnp.minimum(total, blocks) + 2 * GROUP - 1) // (2 * GROUP)
+    lax.fori_loop(0, turns, turn, 0)
+    for k in range(GROUP):
+        second(turns * 2 * GROUP - GROUP + k, keep_b, k, 1.0)
+
+
+def pack6(parts):
+    return jnp.concatenate([p.astype(F32) for p in parts], axis=0).astype(BF16)
 
 
 def contact(state, seg_all, tile_list, pair_mask, tile_count, stiffness, damping):
@@ -260,13 +286,14 @@
         in_specs=[SMEM, SMEM, VMEM, VMEM, VMEM],
         out_specs=VMEM,
         scratch_shapes=[
-            pltpu.VMEM((seg_blocks, 3, 96, 256), BF16),
+            pltpu.VMEM((seg_blocks, 3, 256, 48), BF16),
             pltpu.VMEM((seg_blocks, 8, 256), F32),
+            pltpu.VMEM((2 * GROUP, 2, 256, 128), BF16),
+            pltpu.VMEM((2 * GROUP, 2, 256, 128), BF16),
         ],
         compiler_params=pltpu.CompilerParams(vmem_limit_bytes=32 << 20),
         name="contact",
     )(tile_list, tile_count, state, seg_all, pair_mask)
-
 
 STIFFNESS = 1.0
 DAMPING = 0.3

time: 597 us -> 374 us (0.63)
  blocking collectives: 217 us -> 70.8 us
  Pallas kernels: 357 us -> 280 us
    all_to_all x2, blocking collectives: 217 us -> 70.8 us  [swap(): return lax.all_to_all(blocks, AXES, split_axis=0, concat_axis=0, tiled=True)]
    pallas_call x1, Pallas kernels: 154 us -> 77.7 us  [contact(): pl.pallas_call(functools.partial(contact_kernel, stiffness=stiffness, dam...]
where the time goes in v2:
time: 374 us; the launch traced here: 372 us
  Pallas kernels  280 us (75%)
  blocking collectives  70.8 us (19%)
  starting transfers between devices  9.48 us (3%)
  waiting for transfers between devices  5.92 us (2%)
  local copies, waits for them, and re-layouts  5.13 us (1%)
    pallas_call x1, Pallas kernels, scatter(): pl.pallas_call(scatter_kernel, out_shape=jax.ShapeDtypeStruct((3, nodes),...  97.9 us
    pallas_call x1, Pallas kernels, pack(): pl.pallas_call(pack_kernel, out_shape=jax.ShapeDtypeStruct((pack_index.sh...  78.5 us
    pallas_call x1, Pallas kernels, contact(): pl.pallas_call(functools.partial(contact_kernel, stiffness=stiffness, dam...  77.7 us
    all_to_all x2, blocking collectives, swap(): return lax.all_to_all(blocks, AXES, split_axis=0, concat_axis=0, tiled=True)  70.8 us
    pallas_call x1, Pallas kernels, features(): pl.pallas_call(features_kernel, out_shape=jax.ShapeDtypeStruct((10, segs)...  25.8 us
  transfers between devices with their start and end apart: 4, of which 2 were waited for; matrix products, arithmetic and copies ran while one was open for 0% of the time, Pallas kernels for 0%

profile of v2, /device:TPU:1, one launch (start us, length us, event | category | flops | bytes accessed | tf_op | source)
XLA Modules:
  0.0 372.1 jit_solution(5160853868919366919)
XLA Ops:
  0.0 0.0 copy-start.1
  0.0 0.9 copy-done.1
  1.0 0.0 copy-start.2
  1.0 1.1 copy-done.2
  2.1 0.0 copy-start.3
  2.1 1.1 copy-done.3
  3.2 0.0 copy-start.4
  3.2 0.9 copy-done.4
  4.1 0.0 copy-start.5
  4.1 0.9 copy-done.5
  5.1 78.5 %pack.1 = f32[512,8,128]{2,1,0:T(8,128)S(1)} custom-call(s32[1,65536]{1,0:T(1,128)S(1)} %copy-done.1, f32[3,49152]{1,0:T(4,128)S(1)} %copy-done.2, f32[3,49152]{1,0:T(4,128)S(1)} %copy-done.3, f32[1,49152]{1,0:T(1,128)S(1)} %bitcast.33, f32[1,49152]{1,0:T(1,128)S(1)} %bitcast.34), custom_call_target="tpu_custom_call" | custom-call | tf_op jit(solution)/shard_map/pack/pallas_call | solution.py:97
  83.6 0.0 copy-start.6
  83.6 41.4 %all_to_all.10.state_ref = f32[512,8,128]{2,1,0:T(8,128)S(1)} all-to-all(f32[512,8,128]{2,1,0:T(8,128)S(1)} %pack.1), channel_id=1, replica_groups=mesh['wide'=16,'narrow'=8] {'wide','narrow'}, dimensions={0} | all-to-all | bytes 4194304 | tf_op jit(solution)/shard_map/all_to_all | solution.py:304
  125.0 0.0 copy-start
  125.0 0.0 copy-start.7
  125.0 0.0 copy-done.6
  125.0 25.8 %features.1 = f32[10,2048]{1,0:T(8,128)S(1)} custom-call(s32[4,2048]{1,0:T(4,128)S(1)} %bitcast.35, f32[512,8,128]{2,1,0:T(8,128)S(1)} %all_to_all.10.state_ref), custom_call_target="tpu_custom_call" | custom-call | tf_op jit(solution)/shard_map/features/pallas_call | solution.py:184
  150.8 2.3 collective-permute-start
  153.1 1.3 collective-permute-start.1
  155.0 0.0 collective-permute-done
  155.0 2.7 collective-permute-done.1
  157.8 3.2 collective-permute-start.2
  161.0 2.7 collective-permute-start.3
  163.7 0.0 collective-permute-done.2
  163.7 3.2 collective-permute-done.3
  167.0 0.0 copy-done
  167.0 0.0 copy-done.7
  167.0 77.7 %contact.1 = f32[512,4,128]{2,1,0:T(4,128)S(1)} custom-call(s32[2,1024]{1,0:T(2,128)S(1)} %copy-done.7, s32[1]{0:T(128)S(6)} %copy.18.count_ref, f32[512,8,128]{2,1,0:T(8,128)S(1)} %all_to_all.10.state_ref, f32[10,6144]{1,0:T(8,128)S(1)} %fusion.seg_ref, s32[1024,256]{1,0:T(8,128)S(1)} %copy-done), custom_call_target="tpu_custom_call" | custom-call | tf_op jit(solution)/shard_map/contact/pallas_call | solution.py:283
  244.7 29.5 %all_to_all.11.force_ref = f32[512,4,128]{2,1,0:T(4,128)S(1)} all-to-all(f32[512,4,128]{2,1,0:T(4,128)S(1)} %contact.1), channel_id=1, replica_groups=mesh['wide'=16,'narrow'=8] {'wide','narrow'}, dimensions={0} | all-to-all | bytes 2097152 | tf_op jit(solution)/shard_map/all_to_all | solution.py:304
  274.1 97.9 %scatter.1 = f32[3,49152]{1,0:T(4,128)} custom-call(s32[1,65536]{1,0:T(1,128)S(1)} %copy-done.1, f32[512,4,128]{2,1,0:T(4,128)S(1)} %all_to_all.11.force_ref), custom_call_target="tpu_custom_call" | custom-call | tf_op jit(solution)/shard_map/scatter/pallas_call | solution.py:133
  (11 shorter events, 0.1 us)
Async XLA Ops:
  0.0 0.9 copy-start.1
  1.0 1.1 copy-start.2
  2.1 1.1 copy-start.3
  3.2 0.9 copy-start.4
  4.1 0.9 copy-start.5
  83.6 41.4 %copy-start.6 = (s32[2048,4]{0,1:T(4,128)S(1)}, s32[2048,4]{0,1:T(4,128)}, u32[]{:S(2)}) copy-start(s32[2048,4]{0,1:T(4,128)} %param.14) | copy-start | bytes 98308
  125.0 42.0 %copy-start = (s32[1024,256]{1,0:T(8,128)S(1)}, s32[1024,256]{1,0:T(8,128)}, u32[]{:S(2)}) copy-start(s32[1024,256]{1,0:T(8,128)} %mask_ref.1) | copy-start | bytes 3145732
  125.0 42.0 %copy-start.7 = (s32[2,1024]{1,0:T(2,128)S(1)}, s32[2,1024]{1,0:T(2,128)}, u32[]{:S(2)}) copy-start(s32[2,1024]{1,0:T(2,128)} %tiles_ref.1) | copy-start | bytes 24580
  150.8 4.3 %collective-permute-start = (f32[1,1,10,512]{3,2,1,0:T(8,128)S(1)}, f32[1,1,10,512]{3,2,1,0:T(8,128)S(1)}, u32[]{:S(2)}, u32[]{:S(2)}) collective-permute-start(f32[1,1,10,512]{3,2,1,0:T(8,128)S(1)} %slice_bitcast_fusion.6), channel_id=1, source_target_pairs={{0,8},{8,16},{16,24},{24,32},{32,40},{40,48},{48,56},{56,64},{64,7... | collective-permute-start | bytes 61448 | tf_op jit(solution)/shard_map/ppermute | solution.py:312
  153.1 4.7 %collective-permute-start.1 = (f32[1,1,10,512]{3,2,1,0:T(8,128)S(1)}, f32[1,1,10,512]{3,2,1,0:T(8,128)S(1)}, u32[]{:S(2)}, u32[]{:S(2)}) collective-permute-start(f32[1,1,10,512]{3,2,1,0:T(8,128)S(1)} %slice_bitcast_fusion.6), channel_id=1, source_target_pairs={{8,0},{16,8},{24,16},{32,24},{40,32},{48,40},{56,48},{64,56},{72,6... | collective-permute-start | bytes 61448 | tf_op jit(solution)/shard_map/ppermute | solution.py:313
  157.8 5.9 %collective-permute-start.2 = (f32[3,1,10,512]{3,2,1,0:T(8,128)S(1)}, f32[3,1,10,512]{3,2,1,0:T(8,128)S(1)}, u32[]{:S(2)}, u32[]{:S(2)}) collective-permute-start(f32[3,1,10,512]{3,2,1,0:T(8,128)S(1)} %pad_maximum_fusion), channel_id=1, source_target_pairs={{0,1},{1,2},{2,3},{3,4},{4,5},{5,6},{6,7},{8,9},{9,10},{10,11},{11... | collective-permute-start | bytes 184328 | tf_op jit(solution)/shard_map/ppermute | solution.py:312
  161.0 5.9 %collective-permute-start.3 = (f32[3,1,10,512]{3,2,1,0:T(8,128)S(1)}, f32[3,1,10,512]{3,2,1,0:T(8,128)S(1)}, u32[]{:S(2)}, u32[]{:S(2)}) collective-permute-start(f32[3,1,10,512]{3,2,1,0:T(8,128)S(1)} %pad_maximum_fusion), channel_id=1, source_target_pairs={{1,0},{2,1},{3,2},{4,3},{5,4},{6,5},{7,6},{9,8},{10,9},{11,10},{12... | collective-permute-start | bytes 184328 | tf_op jit(solution)/shard_map/ppermute | solution.py:313

commit v3 on v2

--- a/solution.py
+++ b/solution.py
@@ -9,7 +9,8 @@
 F32 = jnp.float32
 BF16 = jnp.bfloat16
 I32 = jnp.int32
-CHUNK = 256
+CHUNK = 512
+UNR = 1
 GROUP = 4
 LOG2E = 1.4426950408889634
 
@@ -57,10 +58,25 @@
 
 def index_chunks(index_ref, body):
     def turn(i, carry):
-        body(i, lambda k: index_ref[0, i * CHUNK + k])
-        return carry
-
-    lax.fori_loop(0, index_ref.shape[1] // CHUNK, turn, 0, unroll=2)
+        body(i, lambda k: index_ref.at[k][i])
+        return carry
+
+    lax.fori_loop(0, index_ref.shape[1], turn, 0, unroll=UNR)
+
+
+def merge_lanes(tiles):
+    lane = iota((8, 128), 1)
+    bit = 1
+    while len(tiles) > 1:
+        odd = (lane & bit) != 0
+        tiles = [jnp.where(odd, tiles[2 * i + 1], tiles[2 * i]) for i in range(len(tiles) // 2)]
+        bit *= 2
+    return tiles[0]
+
+
+def pick_lanes(row_of, lanes, table_ref):
+    spread = jnp.broadcast_to(lanes, (8, 128))
+    return merge_lanes([jnp.take_along_axis(table_ref[row_of(j)], spread, axis=1) for j in range(128)])
 
 
 def pack_kernel(index_ref, pos_ref, vel_ref, mass_ref, thick_ref, out_ref, rows_ref):
@@ -90,6 +106,10 @@
 
 VMEM = pl.BlockSpec(memory_space=pltpu.VMEM)
 SMEM = pl.BlockSpec(memory_space=pltpu.SMEM)
+
+
+def columns(pack_index):
+    return pack_index.reshape(-1, CHUNK).T
 
 
 def pack(positions, velocities, nodal_mass, thickness, pack_index):
@@ -104,19 +124,32 @@
         ],
         compiler_params=pltpu.CompilerParams(vmem_limit_bytes=48 << 20),
         name="pack",
-    )(pack_index, positions, velocities, nodal_mass.reshape(1, -1), thickness.reshape(1, -1))
+    )(columns(pack_index), positions, velocities, nodal_mass.reshape(1, -1), thickness.reshape(1, -1))
 
 
 def scatter_kernel(index_ref, force_ref, out_ref, rows_ref, ex_a, ex_b):
     nodes = out_ref.shape[1]
-
-    def chunk(c, index):
-        for half, ex in enumerate((ex_a, ex_b)):
-            ex[...] = expand_rows(force_ref[c * 2 + half])
-            for j in range(128):
-                rows_ref[pl.ds(index(half * 128 + j), 1), :] = ex[j : j + 1, :]
-
-    index_chunks(index_ref, chunk)
+    chunks = index_ref.shape[1]
+    tiles = CHUNK // 128
+
+    def spread(c, ex_ref):
+        for part in range(tiles):
+            ex_ref[part * 128 : part * 128 + 128] = expand_rows(force_ref[c * tiles + part])
+
+    def place(c, ex_ref):
+        for j in range(CHUNK):
+            rows_ref[pl.ds(index_ref.at[j][c], 1), :] = ex_ref[j : j + 1, :]
+
+    spread(0, ex_a)
+
+    def turn(i, carry):
+        spread(2 * i + 1, ex_b)
+        place(2 * i, ex_a)
+        spread(jnp.minimum(2 * i + 2, chunks - 1), ex_a)
+        place(2 * i + 1, ex_b)
+        return carry
+
+    lax.fori_loop(0, chunks // 2, turn, 0)
 
     def collect(b, carry):
         at = pl.multiple_of(b * 128, 128)
@@ -126,7 +159,7 @@
         out_ref[:, pl.ds(at, 128)] = feature_major(lines)[0:3]
         return carry
 
-    lax.fori_loop(0, nodes // 128, collect, 0, unroll=4)
+    lax.fori_loop(0, nodes // 128, collect, 0, unroll=8)
 
 
 def scatter(force, pack_index, nodes):
@@ -137,27 +170,35 @@
         out_specs=VMEM,
         scratch_shapes=[
             pltpu.VMEM((nodes + 8, 128), F32),
-            pltpu.VMEM((128, 128), F32),
-            pltpu.VMEM((128, 128), F32),
+            pltpu.VMEM((CHUNK, 128), F32),
+            pltpu.VMEM((CHUNK, 128), F32),
         ],
         compiler_params=pltpu.CompilerParams(vmem_limit_bytes=48 << 20),
         name="scatter",
-    )(pack_index, force)
-
-
-def features_kernel(conn_ref, state_ref, out_ref):
+    )(columns(pack_index), force)
+
+
+def merge_lanes(tiles):
     lane = iota((8, 128), 1)
-
+    bit = 1
+    while len(tiles) > 1:
+        odd = (lane & bit) != 0
+        tiles = [jnp.where(odd, tiles[2 * i + 1], tiles[2 * i]) for i in range(len(tiles) // 2)]
+        bit *= 2
+    return tiles[0]
+
+
+def pick_lanes(row_of, lanes, table_ref):
+    spread = jnp.broadcast_to(lanes, (8, 128))
+    return merge_lanes([jnp.take_along_axis(table_ref[row_of(j)], spread, axis=1) for j in range(128)])
+
+
+def features_kernel(row_ref, lane_ref, state_ref, out_ref):
     def chunk(c, carry):
         corner = []
         for i in range(4):
-            found = jnp.zeros((8, 128), F32)
-            for q in range(128):
-                slot = conn_ref[i, c * 128 + q]
-                tile = state_ref[slot >> 7]
-                moved = pltpu.roll(tile, (q - slot) & 127, axis=1)
-                found = jnp.where(lane == q, moved, found)
-            corner.append(found)
+            row_of = lambda q: row_ref.at[i * 128 + q][c]
+            corner.append(pick_lanes(row_of, lane_ref[pl.ds(i, 1), pl.ds(pl.multiple_of(c * 128, 128), 128)], state_ref))
         total = (corner[0] + corner[1] + corner[2] + corner[3]) * 0.25
         centre = total[0:3]
         d1 = corner[2] - corner[0]
@@ -179,16 +220,22 @@
     lax.fori_loop(0, out_ref.shape[1] // 128, chunk, 0)
 
 
+def corner_rows(connectivity):
+    rows = (connectivity >> 7).T.reshape(4, -1, 128)
+    rows = jnp.transpose(rows, (0, 2, 1)).reshape(512, -1)
+    return jnp.pad(rows, ((0, 0), (0, 128 - rows.shape[1])))
+
+
 def features(connectivity, state):
     segs = connectivity.shape[0]
     return pl.pallas_call(
         features_kernel,
         out_shape=jax.ShapeDtypeStruct((10, segs), F32),
-        in_specs=[SMEM, VMEM],
+        in_specs=[SMEM, VMEM, VMEM],
         out_specs=VMEM,
         compiler_params=pltpu.CompilerParams(vmem_limit_bytes=16 << 20),
         name="features",
-    )(connectivity.T, state)
+    )(corner_rows(connectivity), (connectivity & 127).T, state)
 
 
 def contact_kernel(tiles_ref, count_ref, state_ref, seg_ref, mask_ref, out_ref, coef_ref, normal_ref, keep_a, keep_b, *, stiffness, damping):

time: 374 us -> 313 us (0.84)
  Pallas kernels: 280 us -> 205 us
  blocking collectives: 70.8 us -> 41.8 us
  waiting for transfers between devices: 5.92 us -> 33.4 us
  starting transfers between devices: 9.48 us -> 21 us
    pallas_call x1, Pallas kernels: 97.9 us -> 58.5 us  [scatter(): pl.pallas_call(scatter_kernel, out_shape=jax.ShapeDtypeStruct((3, nodes),...]
    all_to_all x2 -> x1, blocking collectives: 70.8 us -> 41.8 us  [swap(): return lax.all_to_all(blocks, AXES, split_axis=0, concat_axis=0, tiled=True)]
    all_to_all x0 -> x1, waiting for transfers between devices: none -> 27.5 us  [swap(): return lax.all_to_all(blocks, AXES, split_axis=0, concat_axis=0, tiled=True)]
    pallas_call x1, Pallas kernels: 78.5 us -> 62 us  [pack(): pl.pallas_call(pack_kernel, out_shape=jax.ShapeDtypeStruct((pack_index.sh...]
    all_to_all x0 -> x1, starting transfers between devices: none -> 11.5 us  [swap(): return lax.all_to_all(blocks, AXES, split_axis=0, concat_axis=0, tiled=True)]
    pallas_call x1, Pallas kernels: 25.8 us -> 15.4 us  [features(): pl.pallas_call(features_kernel, out_shape=jax.ShapeDtypeStruct((10, segs)...]
    pallas_call x1, Pallas kernels: 77.7 us -> 69 us  [contact(): pl.pallas_call(functools.partial(contact_kernel, stiffness=stiffness, dam...]
  transfers between devices with their start and end apart: 4 -> 5, of which waited for: 2 -> 3; matrix products, arithmetic and copies ran while one was open for 0% -> 1% of each run, Pallas kernels for 0% -> 0%
where the time goes in v3:
time: 313 us
  Pallas kernels  205 us (65%)
  blocking collectives  41.8 us (13%)
  waiting for transfers between devices  33.4 us (11%)
  starting transfers between devices  21 us (7%)
  local copies, waits for them, and re-layouts  8.6 us (3%)
    pallas_call x1, Pallas kernels, contact(): pl.pallas_call(functools.partial(contact_kernel, stiffness=stiffness, dam...  69 us
    pallas_call x1, Pallas kernels, pack(): pl.pallas_call(pack_kernel, out_shape=jax.ShapeDtypeStruct((pack_index.sh...  62 us
    pallas_call x1, Pallas kernels, scatter(): pl.pallas_call(scatter_kernel, out_shape=jax.ShapeDtypeStruct((3, nodes),...  58.5 us
    all_to_all x1, blocking collectives, swap(): return lax.all_to_all(blocks, AXES, split_axis=0, concat_axis=0, tiled=True)  41.8 us
    all_to_all x1, waiting for transfers between devices, swap(): return lax.all_to_all(blocks, AXES, split_axis=0, concat_axis=0, tiled=True)  27.5 us
    pallas_call x1, Pallas kernels, features(): pl.pallas_call(features_kernel, out_shape=jax.ShapeDtypeStruct((10, segs)...  15.4 us
    all_to_all x1, starting transfers between devices, swap(): return lax.all_to_all(blocks, AXES, split_axis=0, concat_axis=0, tiled=True)  11.5 us
  transfers between devices with their start and end apart: 5, of which 3 were waited for; matrix products, arithmetic and copies ran while one was open for 1% of the time, Pallas kernels for 0%

profile of v3, /device:TPU:1, one launch (start us, length us, event | category | flops | bytes accessed | tf_op | source)
XLA Modules:
  0.0 312.7 jit_solution(1016136656103678870)
XLA Ops:
  0.0 0.0 copy-start.3
  0.0 0.5 broadcast.5
  0.5 2.2 reduce.3
  2.8 0.1 copy.11
  2.9 0.0 copy-done.3
  2.9 0.0 copy-start.4
  2.9 1.1 copy-done.4
  4.1 0.9 copy-done.5
  5.0 0.9 copy-done.6
  5.9 62.0 %pack.1 = f32[512,8,128]{2,1,0:T(8,128)S(1)} custom-call(s32[512,128]{1,0:T(8,128)S(1)} %bitcast.44, f32[3,49152]{1,0:T(4,128)S(1)} %copy-done.3, f32[3,49152]{1,0:T(4,128)S(1)} %copy-done.4, f32[1,49152]{1,0:T(1,128)S(1)} %bitcast.46, f32[1,49152]{1,0:T(1,128)S(1)} %bitcast.47), custom_call_target="tpu_custom_call" | custom-call | tf_op jit(solution)/shard_map/pack/pallas_call | solution.py:117
  68.0 1.3 copy-done
  69.3 11.5 %all-to-all-start = ((f32[512,8,128]{2,1,0:T(8,128)}), f32[512,8,128]{2,1,0:T(8,128)S(1)}, u32[]{:S(2)}, u32[]{:S(2)}) async-start(f32[512,8,128]{2,1,0:T(8,128)} %copy-done), calls=%async_computation | async-start | bytes 4194304 | tf_op jit(solution)/shard_map/all_to_all | solution.py:351
  80.8 0.0 copy-done.8
  80.8 0.0 copy-start.7
  80.8 0.8 copy.12
  81.7 1.8 pad.4.row_ref
  83.4 27.5 %all-to-all-done.state_ref = f32[512,8,128]{2,1,0:T(8,128)S(1)} async-done(((f32[512,8,128]{2,1,0:T(8,128)}), f32[512,8,128]{2,1,0:T(8,128)S(1)}, u32[]{:S(2)}, u32[]{:S(2)}) %all-to-all-start) | async-done | bytes 2097184 | tf_op jit(solution)/shard_map/all_to_all | solution.py:351
  110.9 0.9 copy-done.2
  111.8 15.4 %features.1 = f32[10,2048]{1,0:T(8,128)S(1)} custom-call(s32[512,128]{1,0:T(8,128)S(1)} %copy-done.2, s32[4,2048]{1,0:T(4,128)S(1)} %get-tuple-element.5.lane_ref, f32[512,8,128]{2,1,0:T(8,128)S(1)} %all-to-all-done.state_ref), custom_call_target="tpu_custom_call" | custom-call | tf_op jit(solution)/shard_map/features/pallas_call | solution.py:231
  127.3 2.3 collective-permute-start
  129.6 1.3 collective-permute-start.1
  131.5 0.0 collective-permute-done
  131.5 2.7 collective-permute-done.1
  134.3 3.2 %collective-permute-start.2 = (f32[3,1,10,512]{3,2,1,0:T(8,128)S(1)}, f32[3,1,10,512]{3,2,1,0:T(8,128)S(1)}, u32[]{:S(2)}, u32[]{:S(2)}) collective-permute-start(f32[3,1,10,512]{3,2,1,0:T(8,128)S(1)} %pad_maximum_fusion), channel_id=1, source_target_pairs={{0,1},{1,2},{2,3},{3,4},{4,5},{5,6},{6,7},{8,9},{9,10},{10,11},{11... | collective-permute-start | bytes 184328 | tf_op jit(solution)/shard_map/ppermute | solution.py:359
  137.5 2.7 collective-permute-start.3
  140.2 0.0 collective-permute-done.2
  140.2 3.2 %collective-permute-done.3 = f32[3,1,10,512]{3,2,1,0:T(8,128)S(1)} collective-permute-done((f32[3,1,10,512]{3,2,1,0:T(8,128)S(1)}, f32[3,1,10,512]{3,2,1,0:T(8,128)S(1)}, u32[]{:S(2)}, u32[]{:S(2)}) %collective-permute-start.3) | collective-permute-done | bytes 61472 | tf_op jit(solution)/shard_map/ppermute | solution.py:360
  143.5 0.0 copy-done.7
  143.5 0.0 copy-done.1
  143.5 69.0 %contact.1 = f32[512,4,128]{2,1,0:T(4,128)S(1)} custom-call(s32[2,1024]{1,0:T(2,128)S(1)} %copy-done.7, s32[1]{0:T(128)S(6)} %copy.24.count_ref, f32[512,8,128]{2,1,0:T(8,128)S(1)} %all-to-all-done.state_ref, f32[10,6144]{1,0:T(8,128)S(1)} %fusion.seg_ref, s32[1024,256]{1,0:T(8,128)S(1)} %copy-done.1), custom_call_target="tpu_custom_call" | custom-call | tf_op jit(solution)/shard_map/contact/pallas_call | solution.py:330
  212.5 41.8 %all_to_all.10.force_ref = f32[512,4,128]{2,1,0:T(4,128)S(1)} all-to-all(f32[512,4,128]{2,1,0:T(4,128)S(1)} %contact.1), channel_id=1, replica_groups=mesh['wide'=16,'narrow'=8] {'wide','narrow'}, dimensions={0} | all-to-all | bytes 2097152 | tf_op jit(solution)/shard_map/all_to_all | solution.py:351
  254.3 58.5 %scatter.1 = f32[3,49152]{1,0:T(4,128)} custom-call(s32[512,128]{1,0:T(8,128)S(1)} %bitcast.45, f32[512,4,128]{2,1,0:T(4,128)S(1)} %all_to_all.10.force_ref), custom_call_target="tpu_custom_call" | custom-call | tf_op jit(solution)/shard_map/scatter/pallas_call | solution.py:166
  (20 shorter events, 0.1 us)
Async XLA Ops:
  0.0 2.9 copy-start.3
  2.9 1.1 copy-start.4
  4.1 0.9 copy-start.5
  5.0 0.9 copy-start.6
  68.0 1.3 copy-start
  69.3 11.5 %copy-start.8 = (s32[2048,4]{0,1:T(4,128)S(1)}, s32[2048,4]{0,1:T(4,128)}, u32[]{:S(2)}) copy-start(s32[2048,4]{0,1:T(4,128)} %param.14) | copy-start | bytes 98308
  69.3 41.6 %all-to-all-start = ((f32[512,8,128]{2,1,0:T(8,128)}), f32[512,8,128]{2,1,0:T(8,128)S(1)}, u32[]{:S(2)}, u32[]{:S(2)}) async-start(f32[512,8,128]{2,1,0:T(8,128)} %copy-done), calls=%async_computation | async-start | bytes 4194304 | tf_op jit(solution)/shard_map/all_to_all | solution.py:351
  80.8 62.7 %copy-start.7 = (s32[2,1024]{1,0:T(2,128)S(1)}, s32[2,1024]{1,0:T(2,128)}, u32[]{:S(2)}) copy-start(s32[2,1024]{1,0:T(2,128)} %tiles_ref.1) | copy-start | bytes 24580
  81.7 61.8 %copy-start.1 = (s32[1024,256]{1,0:T(8,128)S(1)}, s32[1024,256]{1,0:T(8,128)}, u32[]{:S(2)}) copy-start(s32[1024,256]{1,0:T(8,128)} %mask_ref.1) | copy-start | bytes 3145732
  110.9 1.0 copy-start.2
  127.3 4.3 %collective-permute-start = (f32[1,1,10,512]{3,2,1,0:T(8,128)S(1)}, f32[1,1,10,512]{3,2,1,0:T(8,128)S(1)}, u32[]{:S(2)}, u32[]{:S(2)}) collective-permute-start(f32[1,1,10,512]{3,2,1,0:T(8,128)S(1)} %slice_bitcast_fusion.6), channel_id=1, source_target_pairs={{0,8},{8,16},{16,24},{24,32},{32,40},{40,48},{48,56},{56,64},{64,7... | collective-permute-start | bytes 61448 | tf_op jit(solution)/shard_map/ppermute | solution.py:359
  129.6 4.7 %collective-permute-start.1 = (f32[1,1,10,512]{3,2,1,0:T(8,128)S(1)}, f32[1,1,10,512]{3,2,1,0:T(8,128)S(1)}, u32[]{:S(2)}, u32[]{:S(2)}) collective-permute-start(f32[1,1,10,512]{3,2,1,0:T(8,128)S(1)} %slice_bitcast_fusion.6), channel_id=1, source_target_pairs={{8,0},{16,8},{24,16},{32,24},{40,32},{48,40},{56,48},{64,56},{72,6... | collective-permute-start | bytes 61448 | tf_op jit(solution)/shard_map/ppermute | solution.py:360
  134.3 5.9 %collective-permute-start.2 = (f32[3,1,10,512]{3,2,1,0:T(8,128)S(1)}, f32[3,1,10,512]{3,2,1,0:T(8,128)S(1)}, u32[]{:S(2)}, u32[]{:S(2)}) collective-permute-start(f32[3,1,10,512]{3,2,1,0:T(8,128)S(1)} %pad_maximum_fusion), channel_id=1, source_target_pairs={{0,1},{1,2},{2,3},{3,4},{4,5},{5,6},{6,7},{8,9},{9,10},{10,11},{11... | collective-permute-start | bytes 184328 | tf_op jit(solution)/shard_map/ppermute | solution.py:359
  137.5 5.9 %collective-permute-start.3 = (f32[3,1,10,512]{3,2,1,0:T(8,128)S(1)}, f32[3,1,10,512]{3,2,1,0:T(8,128)S(1)}, u32[]{:S(2)}, u32[]{:S(2)}) collective-permute-start(f32[3,1,10,512]{3,2,1,0:T(8,128)S(1)} %pad_maximum_fusion), channel_id=1, source_target_pairs={{1,0},{2,1},{3,2},{4,3},{5,4},{6,5},{7,6},{9,8},{10,9},{11,10},{12... | collective-permute-start | bytes 184328 | tf_op jit(solution)/shard_map/ppermute | solution.py:360

commit v4 on v3

--- a/solution.py
+++ b/solution.py
@@ -79,8 +79,74 @@
     return merge_lanes([jnp.take_along_axis(table_ref[row_of(j)], spread, axis=1) for j in range(128)])
 
 
-def pack_kernel(index_ref, pos_ref, vel_ref, mass_ref, thick_ref, out_ref, rows_ref):
+WIDE, NARROW = "wide", "narrow"
+
+
+def my_place():
+    wide, narrow = lax.axis_index(WIDE), lax.axis_index(NARROW)
+    return wide // 4, wide % 4, narrow // 2, narrow % 2
+
+
+def my_number():
+    return lax.axis_index(WIDE) * 8 + lax.axis_index(NARROW)
+
+
+def peer(i):
+    z, x, y, core = my_place()
+    dz = i % 4
+    dx = (i // 4 + i) % 4
+    dy = (i // 16 + i // 4 + i) % 4
+    dc = (i // 64) % 2
+    return ((z + dz) % 4) * 4 + (x + dx) % 4, ((y + dy) % 4) * 2 + (core + dc) % 2
+
+
+def greet(barrier, peers):
+    def one(i, carry):
+        pl.semaphore_signal(barrier, inc=1, device_id=peer(i), device_id_type=pl.DeviceIdType.MESH)
+        return carry
+
+    lax.fori_loop(1, peers, one, 0)
+
+
+def block_copy(source_ref, target_ref, send_sem, recv_sem, i):
+    wide, narrow = peer(i)
+    number = wide * 8 + narrow
+    return pltpu.make_async_remote_copy(
+        src_ref=source_ref.at[number],
+        dst_ref=target_ref.at[my_number()],
+        send_sem=send_sem.at[number],
+        recv_sem=recv_sem.at[my_number()],
+        device_id=(wide, narrow),
+        device_id_type=pl.DeviceIdType.MESH,
+    )
+
+
+def wait_blocks(source_ref, target_ref, send_sem, recv_sem, peers):
+    def one(i, carry):
+        wide, narrow = peer(i)
+        number = wide * 8 + narrow
+        copy = pltpu.make_async_remote_copy(
+            src_ref=source_ref.at[number],
+            dst_ref=target_ref.at[number],
+            send_sem=send_sem.at[number],
+            recv_sem=recv_sem.at[number],
+            device_id=(wide, narrow),
+            device_id_type=pl.DeviceIdType.MESH,
+        )
+        copy.wait_send()
+        copy.wait_recv()
+        return carry
+
+    lax.fori_loop(1, peers, one, 0)
+
+
+def pack_kernel(
+    index_ref, pos_ref, vel_ref, mass_ref, thick_ref, out_ref, rows_ref, stage_ref, send_sem, recv_sem, own_sem
+):
     nodes = pos_ref.shape[1]
+    peers = out_ref.shape[0]
+    barrier = pltpu.get_barrier_semaphore()
+    greet(barrier, peers)
 
     def fill(b, carry):
         at = pl.ds(pl.multiple_of(b * 128, 128), 128)
@@ -90,18 +156,30 @@
 
     lax.fori_loop(0, nodes // 128, fill, 0, unroll=8)
     rows_ref[nodes : nodes + 8, :] = jnp.zeros((8, 128), F32)
-
-    def chunk(c, index):
-        for half in range(CHUNK // 128):
+    pl.semaphore_wait(barrier, peers - 1)
+
+    def turn(i, carry):
+        wide, narrow = peer((i + 1) % peers)
+        number = wide * 8 + narrow
+        for part in range(CHUNK // 128):
             lines = []
             for r in range(8):
-                got = [
-                    rows_ref[pl.ds(index(half * 128 + k * 8 + r), 8, stride=0), :] for k in range(16)
-                ]
-                lines.append(merge_groups(got, (8, 128)))
-            out_ref[c * (CHUNK // 128) + half] = feature_major(lines)
-
-    index_chunks(index_ref, chunk)
+                got = [rows_ref[pl.ds(index_ref.at[part * 128 + k * 8 + r][number], 1), :] for k in range(16)]
+                lines.append(jnp.broadcast_to(merge_groups(got, (1, 128)), (8, 128)))
+            stage_ref[number, part] = feature_major(lines)
+
+        @pl.when(i > 0)
+        def _():
+            block_copy(stage_ref, out_ref, send_sem, recv_sem, i).start()
+
+        return carry
+
+    lax.fori_loop(0, peers, turn, 0)
+    me = my_number()
+    own = pltpu.make_async_copy(stage_ref.at[me], out_ref.at[me], own_sem)
+    own.start()
+    wait_blocks(stage_ref, out_ref, send_sem, recv_sem, peers)
+    own.wait()
 
 
 VMEM = pl.BlockSpec(memory_space=pltpu.VMEM)
@@ -114,15 +192,20 @@
 
 def pack(positions, velocities, nodal_mass, thickness, pack_index):
     nodes = positions.shape[1]
+    blocks = (pack_index.shape[1] // CHUNK, CHUNK // 128, 8, 128)
     return pl.pallas_call(
         pack_kernel,
-        out_shape=jax.ShapeDtypeStruct((pack_index.shape[1] // 128, 8, 128), F32),
+        out_shape=jax.ShapeDtypeStruct(blocks, F32),
         in_specs=[SMEM, VMEM, VMEM, VMEM, VMEM],
         out_specs=VMEM,
         scratch_shapes=[
             pltpu.VMEM((nodes + 8, 128), F32),
+            pltpu.VMEM(blocks, F32),
+            pltpu.SemaphoreType.DMA((blocks[0],)),
+            pltpu.SemaphoreType.DMA((blocks[0],)),
+            pltpu.SemaphoreType.DMA,
         ],
-        compiler_params=pltpu.CompilerParams(vmem_limit_bytes=48 << 20),
+        compiler_params=pltpu.CompilerParams(vmem_limit_bytes=48 << 20, collective_id=0, has_side_effects=True),
         name="pack",
     )(columns(pack_index), positions, velocities, nodal_mass.reshape(1, -1), thickness.reshape(1, -1))
 
@@ -363,7 +446,7 @@
 
 
 def on_device(positions, velocities, nodal_mass, thickness, pack_index, connectivity, tile_list, pair_mask, tile_count):
-    state = swap(pack(positions, velocities, nodal_mass, thickness, pack_index))
+    state = pack(positions, velocities, nodal_mass, thickness, pack_index).reshape(-1, 8, 128)
     own = features(connectivity, state)
     ghosts = connectivity.shape[0] // 4
     rim = padded(own[None, None, :, :ghosts], (("wide", 0), ("narrow", 1)))

time: 313 us -> 291 us (0.930)
  waiting for transfers between devices: 33.4 us -> 4.97 us
  blocking collectives: 41.8 us -> 54.7 us
  Pallas kernels: 205 us -> 216 us
  starting transfers between devices: 21 us -> 10.1 us
  local copies, waits for them, and re-layouts: 8.6 us -> 0.91 us
    all_to_all x1 -> x0, waiting for transfers between devices: 27.5 us -> none  [swap(): return lax.all_to_all(blocks, AXES, split_axis=0, concat_axis=0, tiled=True)]
    pallas_call x1, Pallas kernels: 62 us -> 87.9 us  [pack(): pl.pallas_call(pack_kernel, out_shape=jax.ShapeDtypeStruct(blocks, F32),...]
    pallas_call x1, Pallas kernels: 69 us -> 54 us  [contact(): pl.pallas_call(functools.partial(contact_kernel, stiffness=stiffness, dam...]
    all_to_all x1, blocking collectives: 41.8 us -> 54.7 us  [swap(): return lax.all_to_all(blocks, AXES, split_axis=0, concat_axis=0, tiled=True)]
    all_to_all x1 -> x0, starting transfers between devices: 11.5 us -> none  [swap(): return lax.all_to_all(blocks, AXES, split_axis=0, concat_axis=0, tiled=True)]
    unnamed x28 -> x22, local copies, waits for them, and re-layouts: 5.84 us -> 0.59 us
  transfers between devices with their start and end apart: 5 -> 4, of which waited for: 3 -> 2; matrix products, arithmetic and copies ran while one was open for 1% -> 0% of each run, Pallas kernels for 0% -> 0%
where the time goes in v4:
time: 291 us; the launch traced here: 290 us
  Pallas kernels  216 us (74%)
  blocking collectives  54.7 us (19%)
  starting transfers between devices  10.1 us (3%)
  waiting for transfers between devices  4.97 us (2%)
  other arithmetic  3.14 us (1%)
    pallas_call x1, Pallas kernels, pack(): pl.pallas_call(pack_kernel, out_shape=jax.ShapeDtypeStruct(blocks, F32),...  87.9 us
    pallas_call x1, Pallas kernels, scatter(): pl.pallas_call(scatter_kernel, out_shape=jax.ShapeDtypeStruct((3, nodes),...  58.5 us
    all_to_all x1, blocking collectives, swap(): return lax.all_to_all(blocks, AXES, split_axis=0, concat_axis=0, tiled=True)  54.7 us
    pallas_call x1, Pallas kernels, contact(): pl.pallas_call(functools.partial(contact_kernel, stiffness=stiffness, dam...  54 us
    pallas_call x1, Pallas kernels, features(): pl.pallas_call(features_kernel, out_shape=jax.ShapeDtypeStruct((10, segs)...  15.4 us
    ppermute x2, starting transfers between devices, padded(): before = lax.ppermute(tail, axis, [(i, i + 1) for i in range(ends)])  6.86 us
  transfers between devices with their start and end apart: 4, of which 2 were waited for; matrix products, arithmetic and copies ran while one was open for 0% of the time, Pallas kernels for 0%

profile of v4, /device:TPU:1, one launch (start us, length us, event | category | flops | bytes accessed | tf_op | source)
XLA Modules:
  0.0 290.5 jit_solution(17982617435101793864)
XLA Ops:
  0.0 0.0 copy-start.4
  0.0 0.0 copy-start.3
  0.0 0.0 copy-start.2
  0.0 0.0 copy-start.1
  0.0 0.9 and_bitcast_fusion
  0.9 0.1 copy.12
  1.1 0.5 broadcast.5
  1.6 2.2 reduce.3
  3.9 0.1 copy.11
  4.0 0.0 copy-done.4
  4.0 0.0 copy-done.3
  4.0 0.0 copy-done.2
  4.0 0.0 copy-done.1
  4.1 87.9 %pack.1 = f32[128,4,8,128]{3,2,1,0:T(8,128)S(1)} custom-call(s32[512,128]{1,0:T(8,128)S(1)} %bitcast.47, f32[3,49152]{1,0:T(4,128)S(1)} %copy-done.1, f32[3,49152]{1,0:T(4,128)S(1)} %copy-done.2, f32[1,49152]{1,0:T(1,128)S(1)} %bitcast.49, f32[1,49152]{1,0:T(1,128)S(1)} %bitcast.50), custom_call_target="tpu_custom_call" | custom-call | tf_op jit(solution)/shard_map/pack/pallas_call | solution.py:196
  92.0 0.0 copy-start
  92.0 0.0 copy-start.5
  92.0 15.4 %features.1 = f32[10,2048]{1,0:T(8,128)S(1)} custom-call(s32[512,128]{1,0:T(8,128)S(1)} %pad.4.row_ref, s32[4,2048]{1,0:T(4,128)S(1)} %get-tuple-element.5.lane_ref, f32[512,8,128]{2,1,0:T(8,128)S(1)} %bitcast.45), custom_call_target="tpu_custom_call" | custom-call | tf_op jit(solution)/shard_map/features/pallas_call | solution.py:314
  107.4 1.3 collective-permute-start.1
  108.7 4.0 %collective-permute-start = (f32[1,1,10,512]{3,2,1,0:T(8,128)S(1)}, f32[1,1,10,512]{3,2,1,0:T(8,128)S(1)}, u32[]{:S(2)}, u32[]{:S(2)}) collective-permute-start(f32[1,1,10,512]{3,2,1,0:T(8,128)S(1)} %slice_bitcast_fusion.6), channel_id=1, source_target_pairs={{0,8},{8,16},{16,24},{24,32},{32,40},{40,48},{48,56},{56,64},{64,7... | collective-permute-start | bytes 61448 | tf_op jit(solution)/shard_map/ppermute | solution.py:442
  112.7 0.0 collective-permute-done.1
  112.7 1.0 collective-permute-done
  113.8 2.9 collective-permute-start.2
  117.3 1.9 collective-permute-start.3
  119.2 0.0 collective-permute-done.2
  119.3 4.0 %collective-permute-done.3 = f32[3,1,10,512]{3,2,1,0:T(8,128)S(1)} collective-permute-done((f32[3,1,10,512]{3,2,1,0:T(8,128)S(1)}, f32[3,1,10,512]{3,2,1,0:T(8,128)S(1)}, u32[]{:S(2)}, u32[]{:S(2)}) %collective-permute-start.3) | collective-permute-done | bytes 61472 | tf_op jit(solution)/shard_map/ppermute | solution.py:443
  123.3 0.0 copy-done
  123.3 0.0 copy-done.5
  123.3 54.0 %contact.1 = f32[512,4,128]{2,1,0:T(4,128)S(1)} custom-call(s32[2,1024]{1,0:T(2,128)S(1)} %copy-done.5, s32[1]{0:T(128)S(6)} %copy.24.count_ref, f32[512,8,128]{2,1,0:T(8,128)S(1)} %bitcast.46, f32[10,6144]{1,0:T(8,128)S(1)} %fusion.seg_ref, s32[1024,256]{1,0:T(8,128)S(1)} %copy-done), custom_call_target="tpu_custom_call" | custom-call | tf_op jit(solution)/shard_map/contact/pallas_call | solution.py:413
  177.3 54.7 %all_to_all.5.force_ref = f32[512,4,128]{2,1,0:T(4,128)S(1)} all-to-all(f32[512,4,128]{2,1,0:T(4,128)S(1)} %contact.1), channel_id=1, replica_groups=mesh['wide'=16,'narrow'=8] {'wide','narrow'}, dimensions={0} | all-to-all | bytes 2097152 | tf_op jit(solution)/shard_map/all_to_all | solution.py:434
  232.0 58.5 %scatter.1 = f32[3,49152]{1,0:T(4,128)} custom-call(s32[512,128]{1,0:T(8,128)S(1)} %bitcast.48, f32[512,4,128]{2,1,0:T(4,128)S(1)} %all_to_all.5.force_ref), custom_call_target="tpu_custom_call" | custom-call | tf_op jit(solution)/shard_map/scatter/pallas_call | solution.py:249
  (14 shorter events, 0.1 us)
Async XLA Ops:
  0.0 4.0 %copy-start.4 = (f32[49152]{0:T(1024)S(1)}, f32[49152]{0:T(1024)}, u32[]{:S(2)}) copy-start(f32[49152]{0:T(1024)} %param.12) | copy-start | bytes 589828
  0.0 4.0 %copy-start.3 = (f32[49152]{0:T(1024)S(1)}, f32[49152]{0:T(1024)}, u32[]{:S(2)}) copy-start(f32[49152]{0:T(1024)} %param.11) | copy-start | bytes 589828
  0.0 4.0 %copy-start.2 = (f32[3,49152]{1,0:T(4,128)S(1)}, f32[3,49152]{1,0:T(4,128)}, u32[]{:S(2)}) copy-start(f32[3,49152]{1,0:T(4,128)} %vel_ref.1) | copy-start | bytes 1769476
  0.0 4.0 %copy-start.1 = (f32[3,49152]{1,0:T(4,128)S(1)}, f32[3,49152]{1,0:T(4,128)}, u32[]{:S(2)}) copy-start(f32[3,49152]{1,0:T(4,128)} %pos_ref.1) | copy-start | bytes 1769476
  92.0 31.3 %copy-start = (s32[1024,256]{1,0:T(8,128)S(1)}, s32[1024,256]{1,0:T(8,128)}, u32[]{:S(2)}) copy-start(s32[1024,256]{1,0:T(8,128)} %mask_ref.1) | copy-start | bytes 3145732
  92.0 31.3 %copy-start.5 = (s32[2,1024]{1,0:T(2,128)S(1)}, s32[2,1024]{1,0:T(2,128)}, u32[]{:S(2)}) copy-start(s32[2,1024]{1,0:T(2,128)} %tiles_ref.1) | copy-start | bytes 24580
  107.4 5.3 %collective-permute-start.1 = (f32[1,1,10,512]{3,2,1,0:T(8,128)S(1)}, f32[1,1,10,512]{3,2,1,0:T(8,128)S(1)}, u32[]{:S(2)}, u32[]{:S(2)}) collective-permute-start(f32[1,1,10,512]{3,2,1,0:T(8,128)S(1)} %slice_bitcast_fusion.6), channel_id=1, source_target_pairs={{8,0},{16,8},{24,16},{32,24},{40,32},{48,40},{56,48},{64,56},{72,6... | collective-permute-start | bytes 61448 | tf_op jit(solution)/shard_map/ppermute | solution.py:443
  108.7 5.0 %collective-permute-start = (f32[1,1,10,512]{3,2,1,0:T(8,128)S(1)}, f32[1,1,10,512]{3,2,1,0:T(8,128)S(1)}, u32[]{:S(2)}, u32[]{:S(2)}) collective-permute-start(f32[1,1,10,512]{3,2,1,0:T(8,128)S(1)} %slice_bitcast_fusion.6), channel_id=1, source_target_pairs={{0,8},{8,16},{16,24},{24,32},{32,40},{40,48},{48,56},{56,64},{64,7... | collective-permute-start | bytes 61448 | tf_op jit(solution)/shard_map/ppermute | solution.py:442
  113.8 5.5 %collective-permute-start.2 = (f32[3,1,10,512]{3,2,1,0:T(8,128)S(1)}, f32[3,1,10,512]{3,2,1,0:T(8,128)S(1)}, u32[]{:S(2)}, u32[]{:S(2)}) collective-permute-start(f32[3,1,10,512]{3,2,1,0:T(8,128)S(1)} %pad_maximum_fusion), channel_id=1, source_target_pairs={{0,1},{1,2},{2,3},{3,4},{4,5},{5,6},{6,7},{8,9},{9,10},{10,11},{11... | collective-permute-start | bytes 184328 | tf_op jit(solution)/shard_map/ppermute | solution.py:442
  117.3 5.9 %collective-permute-start.3 = (f32[3,1,10,512]{3,2,1,0:T(8,128)S(1)}, f32[3,1,10,512]{3,2,1,0:T(8,128)S(1)}, u32[]{:S(2)}, u32[]{:S(2)}) collective-permute-start(f32[3,1,10,512]{3,2,1,0:T(8,128)S(1)} %pad_maximum_fusion), channel_id=1, source_target_pairs={{1,0},{2,1},{3,2},{4,3},{5,4},{6,5},{7,6},{9,8},{10,9},{11,10},{12... | collective-permute-start | bytes 184328 | tf_op jit(solution)/shard_map/ppermute | solution.py:443

commit v5 on v4

--- a/solution.py
+++ b/solution.py
@@ -110,38 +110,34 @@
 
 def block_copy(source_ref, target_ref, send_sem, recv_sem, i):
     wide, narrow = peer(i)
-    number = wide * 8 + narrow
     return pltpu.make_async_remote_copy(
-        src_ref=source_ref.at[number],
+        src_ref=source_ref.at[wide * 8 + narrow],
         dst_ref=target_ref.at[my_number()],
-        send_sem=send_sem.at[number],
-        recv_sem=recv_sem.at[my_number()],
+        send_sem=send_sem,
+        recv_sem=recv_sem,
         device_id=(wide, narrow),
         device_id_type=pl.DeviceIdType.MESH,
     )
 
 
-def wait_blocks(source_ref, target_ref, send_sem, recv_sem, peers):
-    def one(i, carry):
-        wide, narrow = peer(i)
-        number = wide * 8 + narrow
-        copy = pltpu.make_async_remote_copy(
-            src_ref=source_ref.at[number],
-            dst_ref=target_ref.at[number],
-            send_sem=send_sem.at[number],
-            recv_sem=recv_sem.at[number],
-            device_id=(wide, narrow),
-            device_id_type=pl.DeviceIdType.MESH,
-        )
-        copy.wait_send()
-        copy.wait_recv()
-        return carry
-
-    lax.fori_loop(1, peers, one, 0)
+def finish_blocks(source_ref, target_ref, send_sem, recv_sem, peers):
+    me = my_number()
+    target_ref[me] = source_ref[me]
+    rest = pl.ds(0, peers - 1)
+    all_of_them = pltpu.make_async_remote_copy(
+        src_ref=source_ref.at[rest],
+        dst_ref=target_ref.at[rest],
+        send_sem=send_sem,
+        recv_sem=recv_sem,
+        device_id=peer(1),
+        device_id_type=pl.DeviceIdType.MESH,
+    )
+    all_of_them.wait_send()
+    all_of_them.wait_recv()
 
 
 def pack_kernel(
-    index_ref, pos_ref, vel_ref, mass_ref, thick_ref, out_ref, rows_ref, stage_ref, send_sem, recv_sem, own_sem
+    index_ref, pos_ref, vel_ref, mass_ref, thick_ref, out_ref, rows_ref, stage_ref, send_sem, recv_sem
 ):
     nodes = pos_ref.shape[1]
     peers = out_ref.shape[0]
@@ -175,11 +171,7 @@
         return carry
 
     lax.fori_loop(0, peers, turn, 0)
-    me = my_number()
-    own = pltpu.make_async_copy(stage_ref.at[me], out_ref.at[me], own_sem)
-    own.start()
-    wait_blocks(stage_ref, out_ref, send_sem, recv_sem, peers)
-    own.wait()
+    finish_blocks(stage_ref, out_ref, send_sem, recv_sem, peers)
 
 
 VMEM = pl.BlockSpec(memory_space=pltpu.VMEM)
@@ -201,8 +193,7 @@
         scratch_shapes=[
             pltpu.VMEM((nodes + 8, 128), F32),
             pltpu.VMEM(blocks, F32),
-            pltpu.SemaphoreType.DMA((blocks[0],)),
-            pltpu.SemaphoreType.DMA((blocks[0],)),
+            pltpu.SemaphoreType.DMA,
             pltpu.SemaphoreType.DMA,
         ],
         compiler_params=pltpu.CompilerParams(vmem_limit_bytes=48 << 20, collective_id=0, has_side_effects=True),
@@ -293,11 +284,8 @@
         off = [corner[i][0:3] - centre for i in range(4)]
         square = off[0] * off[0] + off[1] * off[1] + off[2] * off[2] + off[3] * off[3]
         spread = (square[0:1] + square[1:2] + square[2:3]) * 0.25
-        at = pl.ds(pl.multiple_of(c * 128, 128), 128)
-        out_ref[0:3, at] = centre
-        out_ref[3:6, at] = jnp.concatenate([w0 / scale, w1 / scale, w2 / scale], axis=0)
-        out_ref[6:9, at] = total[3:6]
-        out_ref[9:10, at] = spread
+        rows = [centre, w0 / scale, w1 / scale, w2 / scale, total[3:6], spread, jnp.zeros((6, 128), F32)]
+        out_ref[:, pl.ds(pl.multiple_of(c * 128, 128), 128)] = jnp.concatenate(rows, axis=0)
         return carry
 
     lax.fori_loop(0, out_ref.shape[1] // 128, chunk, 0)
@@ -313,7 +301,7 @@
     segs = connectivity.shape[0]
     return pl.pallas_call(
         features_kernel,
-        out_shape=jax.ShapeDtypeStruct((10, segs), F32),
+        out_shape=jax.ShapeDtypeStruct((16, segs), F32),
         in_specs=[SMEM, VMEM, VMEM],
         out_specs=VMEM,
         compiler_params=pltpu.CompilerParams(vmem_limit_bytes=16 << 20),
@@ -321,13 +309,85 @@
     )(corner_rows(connectivity), (connectivity & 127).T, state)
 
 
-def contact_kernel(tiles_ref, count_ref, state_ref, seg_ref, mask_ref, out_ref, coef_ref, normal_ref, keep_a, keep_b, *, stiffness, damping):
+AROUND = [(da, db) for da in (-1, 0, 1) for db in (-1, 0, 1) if (da, db) != (0, 0)]
+
+
+def ghost_exchange(own_ref, ghost_ref, send_sem, recv_sem):
+    wide, narrow = lax.axis_index(WIDE), lax.axis_index(NARROW)
+    waits = []
+    for k, (da, db) in enumerate(AROUND):
+        a, b = wide + da, narrow + db
+        inside = (a >= 0) & (a < lax.axis_size(WIDE)) & (b >= 0) & (b < lax.axis_size(NARROW))
+
+        def copy(a=a, b=b, k=k):
+            return pltpu.make_async_remote_copy(
+                src_ref=own_ref.at[:, pl.ds(0, ghost_ref.shape[2])],
+                dst_ref=ghost_ref.at[7 - k],
+                send_sem=send_sem.at[k],
+                recv_sem=recv_sem.at[7 - k],
+                device_id=(a, b),
+                device_id_type=pl.DeviceIdType.MESH,
+            )
+
+        def arrival(a=a, b=b, k=k):
+            return pltpu.make_async_remote_copy(
+                src_ref=own_ref.at[:, pl.ds(0, ghost_ref.shape[2])],
+                dst_ref=ghost_ref.at[k],
+                send_sem=send_sem.at[k],
+                recv_sem=recv_sem.at[k],
+                device_id=(a, b),
+                device_id_type=pl.DeviceIdType.MESH,
+            )
+
+        @pl.when(inside)
+        def _():
+            copy().start()
+
+        @pl.when(jnp.logical_not(inside))
+        def _():
+            ghost_ref[k] = jnp.zeros(ghost_ref.shape[1:], F32)
+
+        waits.append((inside, arrival))
+
+    def finish():
+        for inside, arrival in waits:
+
+            @pl.when(inside)
+            def _():
+                arrival().wait_send()
+                arrival().wait_recv()
+
+    return finish
+
+
+def contact_kernel(
+    tiles_ref,
+    entry_ref,
+    count_ref,
+    state_ref,
+    own_ref,
+    mask_ref,
+    out_ref,
+    coef_ref,
+    normal_ref,
+    keep_a,
+    keep_b,
+    ghost_ref,
+    stage_ref,
+    ghost_send,
+    ghost_recv,
+    send_sem,
+    recv_sem,
+    *,
+    stiffness,
+    damping,
+):
     blocks = state_ref.shape[0]
-    seg_blocks = seg_ref.shape[1] // 256
-    out_ref[...] = jnp.zeros_like(out_ref)
-
-    def prepare(s, carry):
-        f = seg_ref[:, pl.ds(pl.multiple_of(s * 256, 256), 256)]
+    peers = out_ref.shape[0]
+    barrier = pltpu.get_barrier_semaphore()
+    greet(barrier, peers)
+
+    def prepare(s, f):
         n = f[3:6]
         rate = LOG2E / (f[9:10] + 0.25)
         one = jnp.ones((1, 256), F32)
@@ -342,15 +402,36 @@
             high, middle, low = split3(jnp.concatenate(rows + [zero], axis=0))
             coef_ref[s, i] = pack6([high, high, high, middle, middle, low]).T
         high, middle, _ = split3(n)
-        normal_ref[s] = jnp.concatenate([high.astype(F32), middle.astype(F32), zero[0:2]], axis=0)
-        return carry
-
-    lax.fori_loop(0, seg_blocks, prepare, 0)
+        gap = zero[0:1]
+        normal_ref[s] = jnp.concatenate([high.astype(F32), gap, middle.astype(F32), gap], axis=0)
+
+    own_blocks = own_ref.shape[1] // 256
+
+    def prepare_own(s, carry):
+        prepare(s, own_ref[:, pl.ds(pl.multiple_of(s * 256, 256), 256)])
+        return carry
+
+    lax.fori_loop(0, own_blocks, prepare_own, 0)
+    pl.semaphore_wait(barrier, peers - 1)
+    finish_ghosts = ghost_exchange(own_ref, ghost_ref, ghost_send, ghost_recv)
+    keep_b[...] = jnp.zeros_like(keep_b)
+    finish_ghosts()
+
+    def prepare_ghost(k, carry):
+        for half in range(2):
+            prepare(own_blocks + 2 * k + half, ghost_ref[k, :, 256 * half : 256 * half + 256])
+        return carry
+
+    lax.fori_loop(0, ghost_ref.shape[0], prepare_ghost, 0)
     total = count_ref[0]
     row = iota((8, 128), 0)
 
-    def first(t, keep_ref, slot):
-        block = tiles_ref[0, t]
+    def number(h):
+        wide, narrow = peer((h + 1) % peers)
+        return wide * 8 + narrow
+
+    def first(block, keep_ref, slot):
+        t = entry_ref[block]
         node = state_ref[block]
         sq = jnp.sum(jnp.where(row < 3, node * node, 0.0), axis=0, keepdims=True)
         one = jnp.ones((1, 128), F32)
@@ -372,88 +453,93 @@
             keep_ref[2 * slot + half, 0] = top
             keep_ref[2 * slot + half, 1] = (size - top.astype(F32)).astype(BF16)
 
-    def second(t, keep_ref, slot, on):
+    def second(block, keep_ref, slot):
+        t = entry_ref[block]
         force = jnp.zeros((8, 128), F32)
         for half in range(2):
             e = t + half * blocks
-            live = jnp.where(e < total, on, 0.0)
+            live = jnp.where(e < total, 1.0, 0.0)
             mask = mask_ref[pl.ds(e, 1), :].astype(F32) * live
             weights = (normal_ref[tiles_ref[1, e]] * mask).astype(BF16)
             for part in range(2):
                 force += jnp.dot(weights, keep_ref[2 * slot + half, part], preferred_element_type=F32)
-        out_ref[tiles_ref[0, t], 0:3] = force[0:3] + force[3:6]
-
-    keep_b[...] = jnp.zeros_like(keep_b)
+        return force[0:4] + force[4:8]
+
+    def step(h, before, new_ref, old_ref):
+        now, last = number(h), number(before)
+        for k in range(GROUP):
+            first(now * GROUP + k, new_ref, k)
+            stage_ref[last, k] = second(last * GROUP + k, old_ref, k)
+
+    def send(h):
+        block_copy(stage_ref, out_ref, send_sem, recv_sem, h + 1).start()
 
     def turn(i, carry):
-        t = i * (2 * GROUP)
-        before = jnp.maximum(t - GROUP, 0)
-        on = jnp.where(i > 0, 1.0, 0.0)
-        for k in range(GROUP):
-            first(t + k, keep_a, k)
-            second(before + k, keep_b, k, on)
-        for k in range(GROUP):
-            first(t + GROUP + k, keep_b, k)
-            second(t + k, keep_a, k, 1.0)
-        return carry
-
-    turns = (jnp.minimum(total, blocks) + 2 * GROUP - 1) // (2 * GROUP)
-    lax.fori_loop(0, turns, turn, 0)
+        step(2 * i, (2 * i + peers - 1) % peers, keep_a, keep_b)
+
+        @pl.when(i > 0)
+        def _():
+            send(2 * i - 2)
+
+        step(2 * i + 1, 2 * i, keep_b, keep_a)
+
+        @pl.when(i > 0)
+        def _():
+            send(2 * i - 1)
+
+        return carry
+
+    lax.fori_loop(0, peers // 2, turn, 0)
+    me = my_number()
     for k in range(GROUP):
-        second(turns * 2 * GROUP - GROUP + k, keep_b, k, 1.0)
+        stage_ref[me, k] = second(me * GROUP + k, keep_b, k)
+    send(peers - 2)
+    finish_blocks(stage_ref, out_ref, send_sem, recv_sem, peers)
 
 
 def pack6(parts):
     return jnp.concatenate([p.astype(F32) for p in parts], axis=0).astype(BF16)
 
 
-def contact(state, seg_all, tile_list, pair_mask, tile_count, stiffness, damping):
+def contact(state, own, tile_list, pair_mask, tile_count, ghosts):
     blocks = state.shape[0]
-    seg_blocks = seg_all.shape[1] // 256
+    seg_blocks = (own.shape[1] + 8 * ghosts) // 256
+    back = (blocks // GROUP, GROUP, 4, 128)
+    number = jnp.arange(blocks, dtype=I32)
+    entry = jnp.sum(jnp.where(tile_list[0:1, :blocks] == number[:, None], number[None], 0), axis=1)
+    dma = pltpu.SemaphoreType.DMA
     return pl.pallas_call(
-        functools.partial(contact_kernel, stiffness=stiffness, damping=damping),
-        out_shape=jax.ShapeDtypeStruct((blocks, 4, 128), F32),
-        in_specs=[SMEM, SMEM, VMEM, VMEM, VMEM],
+        functools.partial(contact_kernel, stiffness=STIFFNESS, damping=DAMPING),
+        out_shape=jax.ShapeDtypeStruct(back, F32),
+        in_specs=[SMEM, SMEM, SMEM, VMEM, VMEM, VMEM],
         out_specs=VMEM,
         scratch_shapes=[
             pltpu.VMEM((seg_blocks, 3, 256, 48), BF16),
             pltpu.VMEM((seg_blocks, 8, 256), F32),
             pltpu.VMEM((2 * GROUP, 2, 256, 128), BF16),
             pltpu.VMEM((2 * GROUP, 2, 256, 128), BF16),
+            pltpu.VMEM((8, own.shape[0], ghosts), F32),
+            pltpu.VMEM(back, F32),
+            dma((8,)),
+            dma((8,)),
+            dma,
+            dma,
         ],
-        compiler_params=pltpu.CompilerParams(vmem_limit_bytes=32 << 20),
+        compiler_params=pltpu.CompilerParams(vmem_limit_bytes=32 << 20, collective_id=1, has_side_effects=True),
         name="contact",
-    )(tile_list, tile_count, state, seg_all, pair_mask)
+    )(tile_list, entry, tile_count, state, own, pair_mask)
+
 
 STIFFNESS = 1.0
 DAMPING = 0.3
-AXES = ("wide", "narrow")
-
-
-def swap(blocks):
-    return lax.all_to_all(blocks, AXES, split_axis=0, concat_axis=0, tiled=True)
-
-
-def padded(cells, sides):
-    for axis, dim in sides:
-        ends = lax.axis_size(axis) - 1
-        head = lax.slice_in_dim(cells, 0, 1, axis=dim)
-        tail = lax.slice_in_dim(cells, cells.shape[dim] - 1, cells.shape[dim], axis=dim)
-        before = lax.ppermute(tail, axis, [(i, i + 1) for i in range(ends)])
-        after = lax.ppermute(head, axis, [(i + 1, i) for i in range(ends)])
-        cells = jnp.concatenate([before, cells, after], axis=dim)
-    return cells
+AXES = (WIDE, NARROW)
 
 
 def on_device(positions, velocities, nodal_mass, thickness, pack_index, connectivity, tile_list, pair_mask, tile_count):
     state = pack(positions, velocities, nodal_mass, thickness, pack_index).reshape(-1, 8, 128)
     own = features(connectivity, state)
-    ghosts = connectivity.shape[0] // 4
-    rim = padded(own[None, None, :, :ghosts], (("wide", 0), ("narrow", 1)))
-    around = [rim[i, j] for i in range(3) for j in range(3) if (i, j) != (1, 1)]
-    seg_all = jnp.concatenate([own] + around, axis=1)
-    force = contact(state, seg_all, tile_list, pair_mask, tile_count, STIFFNESS, DAMPING)
-    return scatter(swap(force), pack_index, positions.shape[1])
+    force = contact(state, own, tile_list, pair_mask, tile_count, connectivity.shape[0] // 4)
+    return scatter(force.reshape(-1, 4, 128), pack_index, positions.shape[1])
 
 
 def solution(mesh):

time: 291 us -> 283 us (0.973)
  Pallas kernels: 216 us -> 278 us
  blocking collectives: 54.7 us -> 0 us
  starting transfers between devices: 10.1 us -> 0 us
  waiting for transfers between devices: 4.97 us -> 0 us
    pallas_call x2, Pallas kernels: 69.4 us -> 135 us  [the longest x1 120 us: contact(): pl.pallas_call(functools.partial(contact_kernel, stiffness=STIFFNESS, dam...]
    all_to_all x1 -> x0, blocking collectives: 54.7 us -> none  [swap(): return lax.all_to_all(blocks, AXES, split_axis=0, concat_axis=0, tiled=True)]
    ppermute x4 -> x0, starting transfers between devices: 10.1 us -> none  [the longest x2 6.86 us: padded(): before = lax.ppermute(tail, axis, [(i, i + 1) for i in range(ends)])]
    ppermute x4 -> x0, waiting for transfers between devices: 4.97 us -> none  [the longest x2 3.97 us: padded(): after = lax.ppermute(head, axis, [(i + 1, i) for i in range(ends)])]
    pallas_call x1, Pallas kernels: 87.9 us -> 83.8 us  [pack(): pl.pallas_call(pack_kernel, out_shape=jax.ShapeDtypeStruct(blocks, F32),...]
  transfers between devices with their start and end apart: 4 -> 0, of which waited for: 2 -> 0; matrix products, arithmetic and copies ran while one was open for 0% -> 0% of each run, Pallas kernels for 0% -> 0%
where the time goes in v5:
time: 283 us
  Pallas kernels  278 us (98%)
  other arithmetic  3.18 us (1%)
    pallas_call x1, Pallas kernels, contact(): pl.pallas_call(functools.partial(contact_kernel, stiffness=STIFFNESS, dam...  120 us
    pallas_call x1, Pallas kernels, pack(): pl.pallas_call(pack_kernel, out_shape=jax.ShapeDtypeStruct(blocks, F32),...  83.8 us
    pallas_call x1, Pallas kernels, scatter(): pl.pallas_call(scatter_kernel, out_shape=jax.ShapeDtypeStruct((3, nodes),...  58.5 us
    pallas_call x1, Pallas kernels, features(): pl.pallas_call(features_kernel, out_shape=jax.ShapeDtypeStruct((16, segs)...  15.4 us

profile of v5, /device:TPU:1, one launch (start us, length us, event | category | flops | bytes accessed | tf_op | source)
XLA Modules:
  0.0 283.2 jit_solution(9457836252690699754)
XLA Ops:
  0.0 0.0 copy-start.4
  0.0 0.0 copy-start.3
  0.0 0.0 copy-start.2
  0.0 0.0 copy-start.1
  0.8 0.7 slice.3
  1.5 0.2 select_reduce_fusion.entry_ref
  1.7 0.8 and_bitcast_fusion
  2.5 0.1 copy.14
  2.6 0.5 broadcast.5
  3.1 2.2 reduce.3
  5.4 0.1 copy.13
  5.5 0.0 copy-done.4
  5.6 0.0 copy-done.3
  5.6 0.0 copy-done.2
  5.6 0.0 copy-done.1
  5.6 83.8 %pack.1 = f32[128,4,8,128]{3,2,1,0:T(8,128)S(1)} custom-call(s32[512,128]{1,0:T(8,128)S(1)} %bitcast.20, f32[3,49152]{1,0:T(4,128)S(1)} %copy-done.1, f32[3,49152]{1,0:T(4,128)S(1)} %copy-done.2, f32[1,49152]{1,0:T(1,128)S(1)} %bitcast.22, f32[1,49152]{1,0:T(1,128)S(1)} %bitcast.23), custom_call_target="tpu_custom_call" | custom-call | tf_op jit(solution)/shard_map/pack/pallas_call | solution.py:188
  89.4 0.0 copy-start
  89.4 0.0 copy-start.5
  89.4 15.4 %features.1.own_ref = f32[16,2048]{1,0:T(8,128)S(1)} custom-call(s32[512,128]{1,0:T(8,128)S(1)} %pad.4.row_ref, s32[4,2048]{1,0:T(4,128)S(1)} %get-tuple-element.5.lane_ref, f32[512,8,128]{2,1,0:T(8,128)S(1)} %bitcast.17), custom_call_target="tpu_custom_call" | custom-call | tf_op jit(solution)/shard_map/features/pallas_call | solution.py:302
  104.9 0.0 copy-done
  104.9 0.0 copy-done.5
  104.9 119.8 %contact.1 = f32[128,4,4,128]{3,2,1,0:T(4,128)S(1)} custom-call(s32[2,1024]{1,0:T(2,128)S(1)} %copy-done.5, s32[512]{0:T(512)S(1)} %select_reduce_fusion.entry_ref, s32[1]{0:T(128)S(6)} %copy.18.count_ref, f32[512,8,128]{2,1,0:T(8,128)S(1)} %bitcast.18, f32[16,2048]{1,0:T(8,128)S(1)} %features.1.own_ref, s32[1024,256]{1,0:T(8,128)S(1)} %copy-done), custom_call_target="tpu_custom_call" | custom-call | tf_op jit(solution)/shard_map/contact/pallas_call | solution.py:511
  224.7 58.5 %scatter.1 = f32[3,49152]{1,0:T(4,128)} custom-call(s32[512,128]{1,0:T(8,128)S(1)} %bitcast.21, f32[512,4,128]{2,1,0:T(4,128)S(1)} %bitcast.19), custom_call_target="tpu_custom_call" | custom-call | tf_op jit(solution)/shard_map/scatter/pallas_call | solution.py:240
  (3 shorter events, 0.1 us)
Async XLA Ops:
  0.0 5.5 %copy-start.4 = (f32[49152]{0:T(1024)S(1)}, f32[49152]{0:T(1024)}, u32[]{:S(2)}) copy-start(f32[49152]{0:T(1024)} %param.12) | copy-start | bytes 589828
  0.0 5.6 %copy-start.3 = (f32[49152]{0:T(1024)S(1)}, f32[49152]{0:T(1024)}, u32[]{:S(2)}) copy-start(f32[49152]{0:T(1024)} %param.11) | copy-start | bytes 589828
  0.0 5.6 %copy-start.2 = (f32[3,49152]{1,0:T(4,128)S(1)}, f32[3,49152]{1,0:T(4,128)}, u32[]{:S(2)}) copy-start(f32[3,49152]{1,0:T(4,128)} %vel_ref.1) | copy-start | bytes 1769476
  0.0 5.6 %copy-start.1 = (f32[3,49152]{1,0:T(4,128)S(1)}, f32[3,49152]{1,0:T(4,128)}, u32[]{:S(2)}) copy-start(f32[3,49152]{1,0:T(4,128)} %pos_ref.1) | copy-start | bytes 1769476
  89.4 15.5 %copy-start = (s32[1024,256]{1,0:T(8,128)S(1)}, s32[1024,256]{1,0:T(8,128)}, u32[]{:S(2)}) copy-start(s32[1024,256]{1,0:T(8,128)} %mask_ref.1) | copy-start | bytes 3145732
  89.4 15.5 %copy-start.5 = (s32[2,1024]{1,0:T(2,128)S(1)}, s32[2,1024]{1,0:T(2,128)}, u32[]{:S(2)}) copy-start(s32[2,1024]{1,0:T(2,128)} %tiles_ref.1) | copy-start | bytes 24580

commit v6 on v5

--- a/solution.py
+++ b/solution.py
@@ -82,46 +82,38 @@
 WIDE, NARROW = "wide", "narrow"
 
 
-def my_place():
-    wide, narrow = lax.axis_index(WIDE), lax.axis_index(NARROW)
-    return wide // 4, wide % 4, narrow // 2, narrow % 2
-
-
 def my_number():
-    return lax.axis_index(WIDE) * 8 + lax.axis_index(NARROW)
-
-
-def peer(i):
-    z, x, y, core = my_place()
-    dz = i % 4
-    dx = (i // 4 + i) % 4
-    dy = (i // 16 + i // 4 + i) % 4
-    dc = (i // 64) % 2
-    return ((z + dz) % 4) * 4 + (x + dx) % 4, ((y + dy) % 4) * 2 + (core + dc) % 2
-
-
-def greet(barrier, peers):
+    return lax.axis_index(WIDE) * lax.axis_size(NARROW) + lax.axis_index(NARROW)
+
+
+def peer(me, i):
+    return lax.rem(me + 37 * i, lax.axis_size(WIDE) * lax.axis_size(NARROW))
+
+
+def place(number):
+    return lax.div(number, lax.axis_size(NARROW)), lax.rem(number, lax.axis_size(NARROW))
+
+
+def greet(barrier, me, peers):
     def one(i, carry):
-        pl.semaphore_signal(barrier, inc=1, device_id=peer(i), device_id_type=pl.DeviceIdType.MESH)
+        pl.semaphore_signal(barrier, inc=1, device_id=place(peer(me, i)), device_id_type=pl.DeviceIdType.MESH)
         return carry
 
     lax.fori_loop(1, peers, one, 0)
 
 
-def block_copy(source_ref, target_ref, send_sem, recv_sem, i):
-    wide, narrow = peer(i)
-    return pltpu.make_async_remote_copy(
-        src_ref=source_ref.at[wide * 8 + narrow],
-        dst_ref=target_ref.at[my_number()],
+def send_block(source_ref, target_ref, send_sem, recv_sem, me, number):
+    pltpu.make_async_remote_copy(
+        src_ref=source_ref.at[number],
+        dst_ref=target_ref.at[me],
         send_sem=send_sem,
         recv_sem=recv_sem,
-        device_id=(wide, narrow),
+        device_id=place(number),
         device_id_type=pl.DeviceIdType.MESH,
-    )
-
-
-def finish_blocks(source_ref, target_ref, send_sem, recv_sem, peers):
-    me = my_number()
+    ).start()
+
+
+def finish_blocks(source_ref, target_ref, send_sem, recv_sem, me, peers):
     target_ref[me] = source_ref[me]
     rest = pl.ds(0, peers - 1)
     all_of_them = pltpu.make_async_remote_copy(
@@ -129,7 +121,7 @@
         dst_ref=target_ref.at[rest],
         send_sem=send_sem,
         recv_sem=recv_sem,
-        device_id=peer(1),
+        device_id=place(peer(me, 1)),
         device_id_type=pl.DeviceIdType.MESH,
     )
     all_of_them.wait_send()
@@ -141,8 +133,9 @@
 ):
     nodes = pos_ref.shape[1]
     peers = out_ref.shape[0]
+    me = my_number()
     barrier = pltpu.get_barrier_semaphore()
-    greet(barrier, peers)
+    greet(barrier, me, peers)
 
     def fill(b, carry):
         at = pl.ds(pl.multiple_of(b * 128, 128), 128)
@@ -154,24 +147,27 @@
     rows_ref[nodes : nodes + 8, :] = jnp.zeros((8, 128), F32)
     pl.semaphore_wait(barrier, peers - 1)
 
+    def gather(number, part):
+        lines = []
+        for r in range(8):
+            got = [rows_ref[pl.ds(index_ref.at[part * 128 + k * 8 + r][number], 1), :] for k in range(16)]
+            lines.append(jnp.broadcast_to(merge_groups(got, (1, 128)), (8, 128)))
+        stage_ref[number, part] = feature_major(lines)
+
+    for part in range(CHUNK // 128):
+        gather(peer(me, 1), part)
+
     def turn(i, carry):
-        wide, narrow = peer((i + 1) % peers)
-        number = wide * 8 + narrow
-        for part in range(CHUNK // 128):
-            lines = []
-            for r in range(8):
-                got = [rows_ref[pl.ds(index_ref.at[part * 128 + k * 8 + r][number], 1), :] for k in range(16)]
-                lines.append(jnp.broadcast_to(merge_groups(got, (1, 128)), (8, 128)))
-            stage_ref[number, part] = feature_major(lines)
-
-        @pl.when(i > 0)
-        def _():
-            block_copy(stage_ref, out_ref, send_sem, recv_sem, i).start()
-
-        return carry
-
-    lax.fori_loop(0, peers, turn, 0)
-    finish_blocks(stage_ref, out_ref, send_sem, recv_sem, peers)
+        ready = peer(me, i)
+        number = peer(me, i + 1)
+        gather(number, 0)
+        send_block(stage_ref, out_ref, send_sem, recv_sem, me, ready)
+        for part in range(1, CHUNK // 128):
+            gather(number, part)
+        return carry
+
+    lax.fori_loop(1, peers, turn, 0)
+    finish_blocks(stage_ref, out_ref, send_sem, recv_sem, me, peers)
 
 
 VMEM = pl.BlockSpec(memory_space=pltpu.VMEM)
@@ -384,8 +380,9 @@
 ):
     blocks = state_ref.shape[0]
     peers = out_ref.shape[0]
+    me = my_number()
     barrier = pltpu.get_barrier_semaphore()
-    greet(barrier, peers)
+    greet(barrier, me, peers)
 
     def prepare(s, f):
         n = f[3:6]
@@ -414,7 +411,6 @@
     lax.fori_loop(0, own_blocks, prepare_own, 0)
     pl.semaphore_wait(barrier, peers - 1)
     finish_ghosts = ghost_exchange(own_ref, ghost_ref, ghost_send, ghost_recv)
-    keep_b[...] = jnp.zeros_like(keep_b)
     finish_ghosts()
 
     def prepare_ghost(k, carry):
@@ -425,10 +421,6 @@
     lax.fori_loop(0, ghost_ref.shape[0], prepare_ghost, 0)
     total = count_ref[0]
     row = iota((8, 128), 0)
-
-    def number(h):
-        wide, narrow = peer((h + 1) % peers)
-        return wide * 8 + narrow
 
     def first(block, keep_ref, slot):
         t = entry_ref[block]
@@ -465,36 +457,29 @@
                 force += jnp.dot(weights, keep_ref[2 * slot + half, part], preferred_element_type=F32)
         return force[0:4] + force[4:8]
 
-    def step(h, before, new_ref, old_ref):
-        now, last = number(h), number(before)
+    def step(now, last, new_ref, old_ref, send=None):
         for k in range(GROUP):
             first(now * GROUP + k, new_ref, k)
-            stage_ref[last, k] = second(last * GROUP + k, old_ref, k)
-
-    def send(h):
-        block_copy(stage_ref, out_ref, send_sem, recv_sem, h + 1).start()
+            if last is not None:
+                stage_ref[last, k] = second(last * GROUP + k, old_ref, k)
+            if k == 0 and send is not None:
+                send_block(stage_ref, out_ref, send_sem, recv_sem, me, send)
+
+    step(peer(me, 1), None, keep_a, keep_b)
+    step(peer(me, 2), peer(me, 1), keep_b, keep_a)
 
     def turn(i, carry):
-        step(2 * i, (2 * i + peers - 1) % peers, keep_a, keep_b)
-
-        @pl.when(i > 0)
-        def _():
-            send(2 * i - 2)
-
-        step(2 * i + 1, 2 * i, keep_b, keep_a)
-
-        @pl.when(i > 0)
-        def _():
-            send(2 * i - 1)
-
-        return carry
-
-    lax.fori_loop(0, peers // 2, turn, 0)
-    me = my_number()
+        a, b, c, d = (peer(me, 2 * i + j) for j in (-1, 0, 1, 2))
+        step(c, b, keep_a, keep_b, a)
+        step(d, c, keep_b, keep_a, b)
+        return carry
+
+    lax.fori_loop(1, peers // 2, turn, 0)
+    last = peer(me, peers - 1)
     for k in range(GROUP):
         stage_ref[me, k] = second(me * GROUP + k, keep_b, k)
-    send(peers - 2)
-    finish_blocks(stage_ref, out_ref, send_sem, recv_sem, peers)
+    send_block(stage_ref, out_ref, send_sem, recv_sem, me, last)
+    finish_blocks(stage_ref, out_ref, send_sem, recv_sem, me, peers)
 
 
 def pack6(parts):

time: 283 us -> 276 us (0.975)
  Pallas kernels: 278 us -> 271 us
    pallas_call x1, Pallas kernels: 120 us -> 115 us  [contact(): pl.pallas_call(functools.partial(contact_kernel, stiffness=STIFFNESS, dam...]
where the time goes in v6:
time: 276 us
  Pallas kernels  271 us (98%)
  other arithmetic  3.18 us (1%)
    pallas_call x1, Pallas kernels, contact(): pl.pallas_call(functools.partial(contact_kernel, stiffness=STIFFNESS, dam...  115 us
    pallas_call x1, Pallas kernels, pack(): pl.pallas_call(pack_kernel, out_shape=jax.ShapeDtypeStruct(blocks, F32),...  81.4 us
    pallas_call x1, Pallas kernels, scatter(): pl.pallas_call(scatter_kernel, out_shape=jax.ShapeDtypeStruct((3, nodes),...  58.5 us
    pallas_call x1, Pallas kernels, features(): pl.pallas_call(features_kernel, out_shape=jax.ShapeDtypeStruct((16, segs)...  15.4 us

profile of v6, /device:TPU:1, one launch (start us, length us, event | category | flops | bytes accessed | tf_op | source)
XLA Modules:
  0.0 276.2 jit_solution(12008601953432248923)
XLA Ops:
  0.0 0.0 copy-start.4
  0.0 0.0 copy-start.3
  0.0 0.0 copy-start.2
  0.0 0.0 copy-start.1
  0.8 0.7 slice.3
  1.5 0.2 select_reduce_fusion.entry_ref
  1.7 0.8 and_bitcast_fusion
  2.5 0.1 copy.14
  2.6 0.5 broadcast.5
  3.1 2.2 reduce.3
  5.4 0.1 copy.13
  5.5 0.0 copy-done.4
  5.6 0.0 copy-done.3
  5.6 0.0 copy-done.2
  5.6 0.0 copy-done.1
  5.6 81.4 %pack.1 = f32[128,4,8,128]{3,2,1,0:T(8,128)S(1)} custom-call(s32[512,128]{1,0:T(8,128)S(1)} %bitcast.20, f32[3,49152]{1,0:T(4,128)S(1)} %copy-done.1, f32[3,49152]{1,0:T(4,128)S(1)} %copy-done.2, f32[1,49152]{1,0:T(1,128)S(1)} %bitcast.22, f32[1,49152]{1,0:T(1,128)S(1)} %bitcast.23), custom_call_target="tpu_custom_call" | custom-call | tf_op jit(solution)/shard_map/pack/pallas_call | solution.py:184
  87.0 0.0 copy-start
  87.0 0.0 copy-start.5
  87.0 15.4 %features.1.own_ref = f32[16,2048]{1,0:T(8,128)S(1)} custom-call(s32[512,128]{1,0:T(8,128)S(1)} %pad.4.row_ref, s32[4,2048]{1,0:T(4,128)S(1)} %get-tuple-element.5.lane_ref, f32[512,8,128]{2,1,0:T(8,128)S(1)} %bitcast.17), custom_call_target="tpu_custom_call" | custom-call | tf_op jit(solution)/shard_map/features/pallas_call | solution.py:298
  102.4 0.0 copy-done
  102.5 0.0 copy-done.5
  102.5 115.2 %contact.1 = f32[128,4,4,128]{3,2,1,0:T(4,128)S(1)} custom-call(s32[2,1024]{1,0:T(2,128)S(1)} %copy-done.5, s32[512]{0:T(512)S(1)} %select_reduce_fusion.entry_ref, s32[1]{0:T(128)S(6)} %copy.18.count_ref, f32[512,8,128]{2,1,0:T(8,128)S(1)} %bitcast.18, f32[16,2048]{1,0:T(8,128)S(1)} %features.1.own_ref, s32[1024,256]{1,0:T(8,128)S(1)} %copy-done), custom_call_target="tpu_custom_call" | custom-call | tf_op jit(solution)/shard_map/contact/pallas_call | solution.py:496
  217.7 58.5 %scatter.1 = f32[3,49152]{1,0:T(4,128)} custom-call(s32[512,128]{1,0:T(8,128)S(1)} %bitcast.21, f32[512,4,128]{2,1,0:T(4,128)S(1)} %bitcast.19), custom_call_target="tpu_custom_call" | custom-call | tf_op jit(solution)/shard_map/scatter/pallas_call | solution.py:236
  (3 shorter events, 0.1 us)
Async XLA Ops:
  0.0 5.5 %copy-start.4 = (f32[49152]{0:T(1024)S(1)}, f32[49152]{0:T(1024)}, u32[]{:S(2)}) copy-start(f32[49152]{0:T(1024)} %param.12) | copy-start | bytes 589828
  0.0 5.6 %copy-start.3 = (f32[49152]{0:T(1024)S(1)}, f32[49152]{0:T(1024)}, u32[]{:S(2)}) copy-start(f32[49152]{0:T(1024)} %param.11) | copy-start | bytes 589828
  0.0 5.6 %copy-start.2 = (f32[3,49152]{1,0:T(4,128)S(1)}, f32[3,49152]{1,0:T(4,128)}, u32[]{:S(2)}) copy-start(f32[3,49152]{1,0:T(4,128)} %vel_ref.1) | copy-start | bytes 1769476
  0.0 5.6 %copy-start.1 = (f32[3,49152]{1,0:T(4,128)S(1)}, f32[3,49152]{1,0:T(4,128)}, u32[]{:S(2)}) copy-start(f32[3,49152]{1,0:T(4,128)} %pos_ref.1) | copy-start | bytes 1769476
  87.0 15.5 %copy-start = (s32[1024,256]{1,0:T(8,128)S(1)}, s32[1024,256]{1,0:T(8,128)}, u32[]{:S(2)}) copy-start(s32[1024,256]{1,0:T(8,128)} %mask_ref.1) | copy-start | bytes 3145732
  87.0 15.5 %copy-start.5 = (s32[2,1024]{1,0:T(2,128)S(1)}, s32[2,1024]{1,0:T(2,128)}, u32[]{:S(2)}) copy-start(s32[2,1024]{1,0:T(2,128)} %tiles_ref.1) | copy-start | bytes 24580

commit v7 on v6

--- a/solution.py
+++ b/solution.py
@@ -94,12 +94,8 @@
     return lax.div(number, lax.axis_size(NARROW)), lax.rem(number, lax.axis_size(NARROW))
 
 
-def greet(barrier, me, peers):
-    def one(i, carry):
-        pl.semaphore_signal(barrier, inc=1, device_id=place(peer(me, i)), device_id_type=pl.DeviceIdType.MESH)
-        return carry
-
-    lax.fori_loop(1, peers, one, 0)
+def greet(barrier, me, i):
+    pl.semaphore_signal(barrier, inc=1, device_id=place(peer(me, i)), device_id_type=pl.DeviceIdType.MESH)
 
 
 def send_block(source_ref, target_ref, send_sem, recv_sem, me, number):
@@ -135,15 +131,25 @@
     peers = out_ref.shape[0]
     me = my_number()
     barrier = pltpu.get_barrier_semaphore()
-    greet(barrier, me, peers)
-
-    def fill(b, carry):
+
+    def fill(b):
         at = pl.ds(pl.multiple_of(b * 128, 128), 128)
         tile = jnp.concatenate([pos_ref[:, at], vel_ref[:, at], mass_ref[:, at], thick_ref[:, at]], axis=0)
         rows_ref[at, :] = expand_rows(tile)
-        return carry
-
-    lax.fori_loop(0, nodes // 128, fill, 0, unroll=8)
+
+    share = 2 * (nodes // 128) // peers
+
+    def fill_and_greet(i, carry):
+        for k in range(share):
+            fill(i * share + k)
+        greet(barrier, me, 2 * i + 1)
+        greet(barrier, me, 2 * i + 2)
+        return carry
+
+    lax.fori_loop(0, peers // 2 - 1, fill_and_greet, 0)
+    greet(barrier, me, peers - 1)
+    for k in range(share):
+        fill((peers // 2 - 1) * share + k)
     rows_ref[nodes : nodes + 8, :] = jnp.zeros((8, 128), F32)
     pl.semaphore_wait(barrier, peers - 1)
 
@@ -263,46 +269,30 @@
     return merge_lanes([jnp.take_along_axis(table_ref[row_of(j)], spread, axis=1) for j in range(128)])
 
 
-def features_kernel(row_ref, lane_ref, state_ref, out_ref):
-    def chunk(c, carry):
-        corner = []
-        for i in range(4):
-            row_of = lambda q: row_ref.at[i * 128 + q][c]
-            corner.append(pick_lanes(row_of, lane_ref[pl.ds(i, 1), pl.ds(pl.multiple_of(c * 128, 128), 128)], state_ref))
-        total = (corner[0] + corner[1] + corner[2] + corner[3]) * 0.25
-        centre = total[0:3]
-        d1 = corner[2] - corner[0]
-        d2 = corner[3] - corner[1]
-        w0 = d1[1:2] * d2[2:3] - d1[2:3] * d2[1:2]
-        w1 = d1[2:3] * d2[0:1] - d1[0:1] * d2[2:3]
-        w2 = d1[0:1] * d2[1:2] - d1[1:2] * d2[0:1]
-        scale = jnp.maximum(jnp.sqrt(w0 * w0 + w1 * w1 + w2 * w2), 1.0)
-        off = [corner[i][0:3] - centre for i in range(4)]
-        square = off[0] * off[0] + off[1] * off[1] + off[2] * off[2] + off[3] * off[3]
-        spread = (square[0:1] + square[1:2] + square[2:3]) * 0.25
-        rows = [centre, w0 / scale, w1 / scale, w2 / scale, total[3:6], spread, jnp.zeros((6, 128), F32)]
-        out_ref[:, pl.ds(pl.multiple_of(c * 128, 128), 128)] = jnp.concatenate(rows, axis=0)
-        return carry
-
-    lax.fori_loop(0, out_ref.shape[1] // 128, chunk, 0)
+def segment_features(c, row_ref, lane_ref, state_ref, out_ref):
+    corner = []
+    for i in range(4):
+        row_of = lambda q: row_ref.at[i * 128 + q][c]
+        corner.append(pick_lanes(row_of, lane_ref[pl.ds(i, 1), pl.ds(pl.multiple_of(c * 128, 128), 128)], state_ref))
+    total = (corner[0] + corner[1] + corner[2] + corner[3]) * 0.25
+    centre = total[0:3]
+    d1 = corner[2] - corner[0]
+    d2 = corner[3] - corner[1]
+    w0 = d1[1:2] * d2[2:3] - d1[2:3] * d2[1:2]
+    w1 = d1[2:3] * d2[0:1] - d1[0:1] * d2[2:3]
+    w2 = d1[0:1] * d2[1:2] - d1[1:2] * d2[0:1]
+    scale = jnp.maximum(jnp.sqrt(w0 * w0 + w1 * w1 + w2 * w2), 1.0)
+    off = [corner[i][0:3] - centre for i in range(4)]
+    square = off[0] * off[0] + off[1] * off[1] + off[2] * off[2] + off[3] * off[3]
+    spread = (square[0:1] + square[1:2] + square[2:3]) * 0.25
+    rows = [centre, w0 / scale, w1 / scale, w2 / scale, total[3:6], spread, jnp.zeros((6, 128), F32)]
+    out_ref[:, pl.ds(pl.multiple_of(c * 128, 128), 128)] = jnp.concatenate(rows, axis=0)
 
 
 def corner_rows(connectivity):
     rows = (connectivity >> 7).T.reshape(4, -1, 128)
     rows = jnp.transpose(rows, (0, 2, 1)).reshape(512, -1)
     return jnp.pad(rows, ((0, 0), (0, 128 - rows.shape[1])))
-
-
-def features(connectivity, state):
-    segs = connectivity.shape[0]
-    return pl.pallas_call(
-        features_kernel,
-        out_shape=jax.ShapeDtypeStruct((16, segs), F32),
-        in_specs=[SMEM, VMEM, VMEM],
-        out_specs=VMEM,
-        compiler_params=pltpu.CompilerParams(vmem_limit_bytes=16 << 20),
-        name="features",
-    )(corner_rows(connectivity), (connectivity & 127).T, state)
 
 
 AROUND = [(da, db) for da in (-1, 0, 1) for db in (-1, 0, 1) if (da, db) != (0, 0)]
@@ -360,10 +350,12 @@
     tiles_ref,
     entry_ref,
     count_ref,
+    row_ref,
+    lane_ref,
     state_ref,
-    own_ref,
     mask_ref,
     out_ref,
+    own_ref,
     coef_ref,
     normal_ref,
     keep_a,
@@ -382,7 +374,27 @@
     peers = out_ref.shape[0]
     me = my_number()
     barrier = pltpu.get_barrier_semaphore()
-    greet(barrier, me, peers)
+
+    def corners(c, carry):
+        segment_features(c, row_ref, lane_ref, state_ref, own_ref)
+        return carry
+
+    ghost_chunks = ghost_ref.shape[2] // 128
+    first_ones = 1 + (peers - 1) % ghost_chunks
+    for i in range(1, first_ones):
+        greet(barrier, me, i)
+    share = (peers - first_ones) // ghost_chunks
+
+    def corners_and_greet(c, carry):
+        for j in range(share):
+            greet(barrier, me, first_ones + c * share + j)
+        return corners(c, carry)
+
+    lax.fori_loop(0, ghost_chunks, corners_and_greet, 0)
+    lax.fori_loop(ghost_chunks, ghost_chunks + 2, corners, 0)
+    pl.semaphore_wait(barrier, peers - 1)
+    finish_ghosts = ghost_exchange(own_ref, ghost_ref, ghost_send, ghost_recv)
+    lax.fori_loop(ghost_chunks + 2, own_ref.shape[1] // 128, corners, 0)
 
     def prepare(s, f):
         n = f[3:6]
@@ -409,8 +421,6 @@
         return carry
 
     lax.fori_loop(0, own_blocks, prepare_own, 0)
-    pl.semaphore_wait(barrier, peers - 1)
-    finish_ghosts = ghost_exchange(own_ref, ghost_ref, ghost_send, ghost_recv)
     finish_ghosts()
 
     def prepare_ghost(k, carry):
@@ -486,9 +496,11 @@
     return jnp.concatenate([p.astype(F32) for p in parts], axis=0).astype(BF16)
 
 
-def contact(state, own, tile_list, pair_mask, tile_count, ghosts):
+def contact(state, connectivity, tile_list, pair_mask, tile_count):
     blocks = state.shape[0]
-    seg_blocks = (own.shape[1] + 8 * ghosts) // 256
+    segs = connectivity.shape[0]
+    ghosts = segs // 4
+    seg_blocks = (segs + 8 * ghosts) // 256
     back = (blocks // GROUP, GROUP, 4, 128)
     number = jnp.arange(blocks, dtype=I32)
     entry = jnp.sum(jnp.where(tile_list[0:1, :blocks] == number[:, None], number[None], 0), axis=1)
@@ -496,14 +508,15 @@
     return pl.pallas_call(
         functools.partial(contact_kernel, stiffness=STIFFNESS, damping=DAMPING),
         out_shape=jax.ShapeDtypeStruct(back, F32),
-        in_specs=[SMEM, SMEM, SMEM, VMEM, VMEM, VMEM],
+        in_specs=[SMEM, SMEM, SMEM, SMEM, VMEM, VMEM, VMEM],
         out_specs=VMEM,
         scratch_shapes=[
+            pltpu.VMEM((16, segs), F32),
             pltpu.VMEM((seg_blocks, 3, 256, 48), BF16),
             pltpu.VMEM((seg_blocks, 8, 256), F32),
             pltpu.VMEM((2 * GROUP, 2, 256, 128), BF16),
             pltpu.VMEM((2 * GROUP, 2, 256, 128), BF16),
-            pltpu.VMEM((8, own.shape[0], ghosts), F32),
+            pltpu.VMEM((8, 16, ghosts), F32),
             pltpu.VMEM(back, F32),
             dma((8,)),
             dma((8,)),
@@ -512,7 +525,7 @@
         ],
         compiler_params=pltpu.CompilerParams(vmem_limit_bytes=32 << 20, collective_id=1, has_side_effects=True),
         name="contact",
-    )(tile_list, entry, tile_count, state, own, pair_mask)
+    )(tile_list, entry, tile_count, corner_rows(connectivity), (connectivity & 127).T, state, pair_mask)
 
 
 STIFFNESS = 1.0
@@ -522,8 +535,7 @@
 
 def on_device(positions, velocities, nodal_mass, thickness, pack_index, connectivity, tile_list, pair_mask, tile_count):
     state = pack(positions, velocities, nodal_mass, thickness, pack_index).reshape(-1, 8, 128)
-    own = features(connectivity, state)
-    force = contact(state, own, tile_list, pair_mask, tile_count, connectivity.shape[0] // 4)
+    force = contact(state, connectivity, tile_list, pair_mask, tile_count)
     return scatter(force.reshape(-1, 4, 128), pack_index, positions.shape[1])
 
 

time: 276 us -> 274 us (level)
  Pallas kernels: 271 us -> 268 us
    pallas_call x1 -> x0, Pallas kernels: 15.4 us -> none  [features(): pl.pallas_call(features_kernel, out_shape=jax.ShapeDtypeStruct((16, segs)...]
    pallas_call x1, Pallas kernels: 115 us -> 123 us  [contact(): pl.pallas_call(functools.partial(contact_kernel, stiffness=STIFFNESS, dam...]
    pallas_call x1, Pallas kernels: 81.4 us -> 86.5 us  [pack(): pl.pallas_call(pack_kernel, out_shape=jax.ShapeDtypeStruct(blocks, F32),...]
where the time goes in v7:
time: 274 us
  Pallas kernels  268 us (98%)
  other arithmetic  3.18 us (1%)
    pallas_call x1, Pallas kernels, contact(): pl.pallas_call(functools.partial(contact_kernel, stiffness=STIFFNESS, dam...  123 us
    pallas_call x1, Pallas kernels, pack(): pl.pallas_call(pack_kernel, out_shape=jax.ShapeDtypeStruct(blocks, F32),...  86.5 us
    pallas_call x1, Pallas kernels, scatter(): pl.pallas_call(scatter_kernel, out_shape=jax.ShapeDtypeStruct((3, nodes),...  58.5 us

profile of v7, /device:TPU:1, one launch (start us, length us, event | category | flops | bytes accessed | tf_op | source)
XLA Modules:
  0.0 273.6 jit_solution(3679924473791470968)
XLA Ops:
  0.0 0.0 copy-start.4
  0.0 0.0 copy-start.3
  0.0 0.0 copy-start.2
  0.0 0.0 copy-start.1
  0.8 0.7 slice.3
  1.5 0.2 select_reduce_fusion.entry_ref
  1.7 0.8 and_bitcast_fusion
  2.5 0.1 copy.14
  2.6 0.5 broadcast.5
  3.1 2.2 reduce.3
  5.4 0.1 copy.13
  5.5 0.0 copy-done.4
  5.6 0.0 copy-done.3
  5.6 0.0 copy-done.2
  5.6 0.0 copy-done.1
  5.6 0.0 copy-start
  5.6 0.0 copy-start.5
  5.6 86.5 %pack.1 = f32[128,4,8,128]{3,2,1,0:T(8,128)S(1)} custom-call(s32[512,128]{1,0:T(8,128)S(1)} %bitcast.19, f32[3,49152]{1,0:T(4,128)S(1)} %copy-done.1, f32[3,49152]{1,0:T(4,128)S(1)} %copy-done.2, f32[1,49152]{1,0:T(1,128)S(1)} %bitcast.21, f32[1,49152]{1,0:T(1,128)S(1)} %bitcast.22), custom_call_target="tpu_custom_call" | custom-call | tf_op jit(solution)/shard_map/pack/pallas_call | solution.py:190
  92.1 0.0 copy-done
  92.2 0.0 copy-done.5
  92.2 123.0 %contact.1 = f32[128,4,4,128]{3,2,1,0:T(4,128)S(1)} custom-call(s32[2,1024]{1,0:T(2,128)S(1)} %copy-done.5, s32[512]{0:T(512)S(1)} %select_reduce_fusion.entry_ref, s32[1]{0:T(128)S(6)} %copy.18.count_ref, s32[512,128]{1,0:T(8,128)S(1)} %pad.4.row_ref, s32[4,2048]{1,0:T(4,128)S(1)} %get-tuple-element.5.lane_ref, f32[512,8,128]{2,1,0:T(8,128)S(1)} %bitcast.17, ...), custom_call_target="tpu_custom_call" | custom-call | tf_op jit(solution)/shard_map/contact/pallas_call | solution.py:508
  215.1 58.5 %scatter.1 = f32[3,49152]{1,0:T(4,128)} custom-call(s32[512,128]{1,0:T(8,128)S(1)} %bitcast.20, f32[512,4,128]{2,1,0:T(4,128)S(1)} %bitcast.18), custom_call_target="tpu_custom_call" | custom-call | tf_op jit(solution)/shard_map/scatter/pallas_call | solution.py:242
  (3 shorter events, 0.1 us)
Async XLA Ops:
  0.0 5.5 %copy-start.4 = (f32[49152]{0:T(1024)S(1)}, f32[49152]{0:T(1024)}, u32[]{:S(2)}) copy-start(f32[49152]{0:T(1024)} %param.12) | copy-start | bytes 589828
  0.0 5.6 %copy-start.3 = (f32[49152]{0:T(1024)S(1)}, f32[49152]{0:T(1024)}, u32[]{:S(2)}) copy-start(f32[49152]{0:T(1024)} %param.11) | copy-start | bytes 589828
  0.0 5.6 %copy-start.2 = (f32[3,49152]{1,0:T(4,128)S(1)}, f32[3,49152]{1,0:T(4,128)}, u32[]{:S(2)}) copy-start(f32[3,49152]{1,0:T(4,128)} %vel_ref.1) | copy-start | bytes 1769476
  0.0 5.6 %copy-start.1 = (f32[3,49152]{1,0:T(4,128)S(1)}, f32[3,49152]{1,0:T(4,128)}, u32[]{:S(2)}) copy-start(f32[3,49152]{1,0:T(4,128)} %pos_ref.1) | copy-start | bytes 1769476
  5.6 86.6 %copy-start = (s32[1024,256]{1,0:T(8,128)S(1)}, s32[1024,256]{1,0:T(8,128)}, u32[]{:S(2)}) copy-start(s32[1024,256]{1,0:T(8,128)} %mask_ref.1) | copy-start | bytes 3145732
  5.6 86.6 %copy-start.5 = (s32[2,1024]{1,0:T(2,128)S(1)}, s32[2,1024]{1,0:T(2,128)}, u32[]{:S(2)}) copy-start(s32[2,1024]{1,0:T(2,128)} %tiles_ref.1) | copy-start | bytes 24580

commit v8 on v7

--- a/solution.py
+++ b/solution.py
@@ -132,47 +132,44 @@
     me = my_number()
     barrier = pltpu.get_barrier_semaphore()
 
-    def fill(b):
+    def greet_one(i, carry):
+        greet(barrier, me, i)
+        return carry
+
+    lax.fori_loop(1, peers, greet_one, 0)
+
+    def fill(b, carry):
         at = pl.ds(pl.multiple_of(b * 128, 128), 128)
         tile = jnp.concatenate([pos_ref[:, at], vel_ref[:, at], mass_ref[:, at], thick_ref[:, at]], axis=0)
         rows_ref[at, :] = expand_rows(tile)
-
-    share = 2 * (nodes // 128) // peers
-
-    def fill_and_greet(i, carry):
-        for k in range(share):
-            fill(i * share + k)
-        greet(barrier, me, 2 * i + 1)
-        greet(barrier, me, 2 * i + 2)
-        return carry
-
-    lax.fori_loop(0, peers // 2 - 1, fill_and_greet, 0)
-    greet(barrier, me, peers - 1)
-    for k in range(share):
-        fill((peers // 2 - 1) * share + k)
+        return carry
+
+    lax.fori_loop(0, nodes // 128, fill, 0, unroll=8)
     rows_ref[nodes : nodes + 8, :] = jnp.zeros((8, 128), F32)
     pl.semaphore_wait(barrier, peers - 1)
 
-    def gather(number, part):
-        lines = []
-        for r in range(8):
-            got = [rows_ref[pl.ds(index_ref.at[part * 128 + k * 8 + r][number], 1), :] for k in range(16)]
-            lines.append(jnp.broadcast_to(merge_groups(got, (1, 128)), (8, 128)))
-        stage_ref[number, part] = feature_major(lines)
-
-    for part in range(CHUNK // 128):
-        gather(peer(me, 1), part)
+    def gather(i):
+        number = peer(me, i)
+        for part in range(CHUNK // 128):
+            lines = []
+            for r in range(8):
+                got = [rows_ref[pl.ds(index_ref.at[part * 128 + k * 8 + r][number], 1), :] for k in range(16)]
+                lines.append(jnp.broadcast_to(merge_groups(got, (1, 128)), (8, 128)))
+            stage_ref[number, part] = feature_major(lines)
+
+    def send(i):
+        send_block(stage_ref, out_ref, send_sem, recv_sem, me, peer(me, i))
+
+    gather(1)
+    gather(2)
 
     def turn(i, carry):
-        ready = peer(me, i)
-        number = peer(me, i + 1)
-        gather(number, 0)
-        send_block(stage_ref, out_ref, send_sem, recv_sem, me, ready)
-        for part in range(1, CHUNK // 128):
-            gather(number, part)
-        return carry
-
-    lax.fori_loop(1, peers, turn, 0)
+        send(i - 1)
+        gather(i + 1)
+        return carry
+
+    lax.fori_loop(2, peers, turn, 0)
+    send(peers - 1)
     finish_blocks(stage_ref, out_ref, send_sem, recv_sem, me, peers)
 
 
@@ -467,28 +464,38 @@
                 force += jnp.dot(weights, keep_ref[2 * slot + half, part], preferred_element_type=F32)
         return force[0:4] + force[4:8]
 
-    def step(now, last, new_ref, old_ref, send=None):
+    def finish(i, old_ref):
+        last = peer(me, i)
+        for k in range(GROUP):
+            stage_ref[last, k] = second(last * GROUP + k, old_ref, k)
+
+    def step(i, new_ref, old_ref):
+        now, last = peer(me, i), peer(me, i - 1)
         for k in range(GROUP):
             first(now * GROUP + k, new_ref, k)
-            if last is not None:
-                stage_ref[last, k] = second(last * GROUP + k, old_ref, k)
-            if k == 0 and send is not None:
-                send_block(stage_ref, out_ref, send_sem, recv_sem, me, send)
-
-    step(peer(me, 1), None, keep_a, keep_b)
-    step(peer(me, 2), peer(me, 1), keep_b, keep_a)
+            stage_ref[last, k] = second(last * GROUP + k, old_ref, k)
+
+    def send(i):
+        send_block(stage_ref, out_ref, send_sem, recv_sem, me, peer(me, i))
+
+    for k in range(GROUP):
+        first(peer(me, 1) * GROUP + k, keep_b, k)
+    step(2, keep_a, keep_b)
+    step(3, keep_b, keep_a)
 
     def turn(i, carry):
-        a, b, c, d = (peer(me, 2 * i + j) for j in (-1, 0, 1, 2))
-        step(c, b, keep_a, keep_b, a)
-        step(d, c, keep_b, keep_a, b)
-        return carry
-
-    lax.fori_loop(1, peers // 2, turn, 0)
-    last = peer(me, peers - 1)
-    for k in range(GROUP):
-        stage_ref[me, k] = second(me * GROUP + k, keep_b, k)
-    send_block(stage_ref, out_ref, send_sem, recv_sem, me, last)
+        send(2 * i - 1)
+        send(2 * i)
+        step(2 * i + 2, keep_a, keep_b)
+        step(2 * i + 3, keep_b, keep_a)
+        return carry
+
+    lax.fori_loop(1, peers // 2 - 1, turn, 0)
+    send(peers - 3)
+    send(peers - 2)
+    step(peers, keep_a, keep_b)
+    finish(peers, keep_a)
+    send(peers - 1)
     finish_blocks(stage_ref, out_ref, send_sem, recv_sem, me, peers)
 
 

time: 274 us -> 244 us (0.89)
  Pallas kernels: 268 us -> 238 us
    pallas_call x1, Pallas kernels: 123 us -> 107 us  [contact(): pl.pallas_call(functools.partial(contact_kernel, stiffness=STIFFNESS, dam...]
    pallas_call x1, Pallas kernels: 86.5 us -> 72.6 us  [pack(): pl.pallas_call(pack_kernel, out_shape=jax.ShapeDtypeStruct(blocks, F32),...]
where the time goes in v8:
time: 244 us; the launch traced here: 243 us
  Pallas kernels  238 us (98%)
  other arithmetic  3.18 us (1%)
    pallas_call x1, Pallas kernels, contact(): pl.pallas_call(functools.partial(contact_kernel, stiffness=STIFFNESS, dam...  107 us
    pallas_call x1, Pallas kernels, pack(): pl.pallas_call(pack_kernel, out_shape=jax.ShapeDtypeStruct(blocks, F32),...  72.6 us
    pallas_call x1, Pallas kernels, scatter(): pl.pallas_call(scatter_kernel, out_shape=jax.ShapeDtypeStruct((3, nodes),...  58.5 us

profile of v8, /device:TPU:1, one launch (start us, length us, event | category | flops | bytes accessed | tf_op | source)
XLA Modules:
  0.0 243.5 jit_solution(10441270182199119889)
XLA Ops:
  0.0 0.0 copy-start.4
  0.0 0.0 copy-start.3
  0.0 0.0 copy-start.2
  0.0 0.0 copy-start.1
  0.8 0.7 slice.3
  1.5 0.2 select_reduce_fusion.entry_ref
  1.7 0.8 and_bitcast_fusion
  2.5 0.1 copy.14
  2.6 0.5 broadcast.5
  3.1 2.2 reduce.3
  5.4 0.1 copy.13
  5.5 0.0 copy-done.4
  5.6 0.0 copy-done.3
  5.6 0.0 copy-done.2
  5.6 0.0 copy-done.1
  5.6 0.0 copy-start
  5.6 0.0 copy-start.5
  5.6 72.6 %pack.1 = f32[128,4,8,128]{3,2,1,0:T(8,128)S(1)} custom-call(s32[512,128]{1,0:T(8,128)S(1)} %bitcast.19, f32[3,49152]{1,0:T(4,128)S(1)} %copy-done.1, f32[3,49152]{1,0:T(4,128)S(1)} %copy-done.2, f32[1,49152]{1,0:T(1,128)S(1)} %bitcast.21, f32[1,49152]{1,0:T(1,128)S(1)} %bitcast.22), custom_call_target="tpu_custom_call" | custom-call | tf_op jit(solution)/shard_map/pack/pallas_call | solution.py:187
  78.2 0.0 copy-done
  78.2 0.0 copy-done.5
  78.3 106.7 %contact.1 = f32[128,4,4,128]{3,2,1,0:T(4,128)S(1)} custom-call(s32[2,1024]{1,0:T(2,128)S(1)} %copy-done.5, s32[512]{0:T(512)S(1)} %select_reduce_fusion.entry_ref, s32[1]{0:T(128)S(6)} %copy.18.count_ref, s32[512,128]{1,0:T(8,128)S(1)} %pad.4.row_ref, s32[4,2048]{1,0:T(4,128)S(1)} %get-tuple-element.5.lane_ref, f32[512,8,128]{2,1,0:T(8,128)S(1)} %bitcast.17, ...), custom_call_target="tpu_custom_call" | custom-call | tf_op jit(solution)/shard_map/contact/pallas_call | solution.py:515
  185.0 58.5 %scatter.1 = f32[3,49152]{1,0:T(4,128)} custom-call(s32[512,128]{1,0:T(8,128)S(1)} %bitcast.20, f32[512,4,128]{2,1,0:T(4,128)S(1)} %bitcast.18), custom_call_target="tpu_custom_call" | custom-call | tf_op jit(solution)/shard_map/scatter/pallas_call | solution.py:239
  (3 shorter events, 0.1 us)
Async XLA Ops:
  0.0 5.5 %copy-start.4 = (f32[49152]{0:T(1024)S(1)}, f32[49152]{0:T(1024)}, u32[]{:S(2)}) copy-start(f32[49152]{0:T(1024)} %param.12) | copy-start | bytes 589828
  0.0 5.6 %copy-start.3 = (f32[49152]{0:T(1024)S(1)}, f32[49152]{0:T(1024)}, u32[]{:S(2)}) copy-start(f32[49152]{0:T(1024)} %param.11) | copy-start | bytes 589828
  0.0 5.6 %copy-start.2 = (f32[3,49152]{1,0:T(4,128)S(1)}, f32[3,49152]{1,0:T(4,128)}, u32[]{:S(2)}) copy-start(f32[3,49152]{1,0:T(4,128)} %vel_ref.1) | copy-start | bytes 1769476
  0.0 5.6 %copy-start.1 = (f32[3,49152]{1,0:T(4,128)S(1)}, f32[3,49152]{1,0:T(4,128)}, u32[]{:S(2)}) copy-start(f32[3,49152]{1,0:T(4,128)} %pos_ref.1) | copy-start | bytes 1769476
  5.6 72.7 %copy-start = (s32[1024,256]{1,0:T(8,128)S(1)}, s32[1024,256]{1,0:T(8,128)}, u32[]{:S(2)}) copy-start(s32[1024,256]{1,0:T(8,128)} %mask_ref.1) | copy-start | bytes 3145732
  5.6 72.7 %copy-start.5 = (s32[2,1024]{1,0:T(2,128)S(1)}, s32[2,1024]{1,0:T(2,128)}, u32[]{:S(2)}) copy-start(s32[2,1024]{1,0:T(2,128)} %tiles_ref.1) | copy-start | bytes 24580

commit v9 on v8

--- a/solution.py
+++ b/solution.py
@@ -164,11 +164,13 @@
     gather(2)
 
     def turn(i, carry):
-        send(i - 1)
-        gather(i + 1)
-        return carry
-
-    lax.fori_loop(2, peers, turn, 0)
+        send(2 * i - 1)
+        send(2 * i)
+        gather(2 * i + 1)
+        gather(2 * i + 2)
+        return carry
+
+    lax.fori_loop(1, peers // 2, turn, 0)
     send(peers - 1)
     finish_blocks(stage_ref, out_ref, send_sem, recv_sem, me, peers)
 
@@ -478,24 +480,29 @@
     def send(i):
         send_block(stage_ref, out_ref, send_sem, recv_sem, me, peer(me, i))
 
+    keep = (keep_a, keep_b)
     for k in range(GROUP):
         first(peer(me, 1) * GROUP + k, keep_b, k)
-    step(2, keep_a, keep_b)
-    step(3, keep_b, keep_a)
+    for j in range(2, 6):
+        step(j, keep[j % 2], keep[1 - j % 2])
+    turns = (peers - 6) // 4
 
     def turn(i, carry):
-        send(2 * i - 1)
-        send(2 * i)
-        step(2 * i + 2, keep_a, keep_b)
-        step(2 * i + 3, keep_b, keep_a)
-        return carry
-
-    lax.fori_loop(1, peers // 2 - 1, turn, 0)
-    send(peers - 3)
-    send(peers - 2)
-    step(peers, keep_a, keep_b)
-    finish(peers, keep_a)
-    send(peers - 1)
+        for j in range(4):
+            send(4 * i + 1 + j)
+        for j in range(4):
+            step(4 * i + 6 + j, keep[j % 2], keep[1 - j % 2])
+        return carry
+
+    lax.fori_loop(0, turns, turn, 0)
+    sent = 4 * turns
+    for j in range(sent + 1, sent + 5):
+        send(j)
+    for j in range(sent + 6, peers + 1):
+        step(j, keep[j % 2], keep[1 - j % 2])
+    finish(peers, keep[peers % 2])
+    for j in range(sent + 5, peers):
+        send(j)
     finish_blocks(stage_ref, out_ref, send_sem, recv_sem, me, peers)
 
 

time: 244 us -> 235 us (0.963)
  Pallas kernels: 238 us -> 230 us
    pallas_call x1, Pallas kernels: 72.6 us -> 68 us  [pack(): pl.pallas_call(pack_kernel, out_shape=jax.ShapeDtypeStruct(blocks, F32),...]
    pallas_call x1, Pallas kernels: 107 us -> 103 us  [contact(): pl.pallas_call(functools.partial(contact_kernel, stiffness=STIFFNESS, dam...]
where the time goes in v9:
time: 235 us
  Pallas kernels  230 us (98%)
  other arithmetic  3.18 us (1%)
    pallas_call x1, Pallas kernels, contact(): pl.pallas_call(functools.partial(contact_kernel, stiffness=STIFFNESS, dam...  103 us
    pallas_call x1, Pallas kernels, pack(): pl.pallas_call(pack_kernel, out_shape=jax.ShapeDtypeStruct(blocks, F32),...  68 us
    pallas_call x1, Pallas kernels, scatter(): pl.pallas_call(scatter_kernel, out_shape=jax.ShapeDtypeStruct((3, nodes),...  58.5 us

profile of v9, /device:TPU:1, one launch (start us, length us, event | category | flops | bytes accessed | tf_op | source)
XLA Modules:
  0.0 235.3 jit_solution(17032418313447853224)
XLA Ops:
  0.0 0.0 copy-start.4
  0.0 0.0 copy-start.3
  0.0 0.0 copy-start.2
  0.0 0.0 copy-start.1
  0.8 0.7 slice.3
  1.5 0.2 select_reduce_fusion.entry_ref
  1.7 0.8 and_bitcast_fusion
  2.5 0.1 copy.14
  2.6 0.5 broadcast.5
  3.1 2.2 reduce.3
  5.4 0.1 copy.13
  5.5 0.0 copy-done.4
  5.6 0.0 copy-done.3
  5.6 0.0 copy-done.2
  5.6 0.0 copy-done.1
  5.6 0.0 copy-start
  5.6 0.0 copy-start.5
  5.6 68.0 %pack.1 = f32[128,4,8,128]{3,2,1,0:T(8,128)S(1)} custom-call(s32[512,128]{1,0:T(8,128)S(1)} %bitcast.19, f32[3,49152]{1,0:T(4,128)S(1)} %copy-done.1, f32[3,49152]{1,0:T(4,128)S(1)} %copy-done.2, f32[1,49152]{1,0:T(1,128)S(1)} %bitcast.21, f32[1,49152]{1,0:T(1,128)S(1)} %bitcast.22), custom_call_target="tpu_custom_call" | custom-call | tf_op jit(solution)/shard_map/pack/pallas_call | solution.py:189
  73.7 0.0 copy-done
  73.7 0.0 copy-done.5
  73.7 103.1 %contact.1 = f32[128,4,4,128]{3,2,1,0:T(4,128)S(1)} custom-call(s32[2,1024]{1,0:T(2,128)S(1)} %copy-done.5, s32[512]{0:T(512)S(1)} %select_reduce_fusion.entry_ref, s32[1]{0:T(128)S(6)} %copy.18.count_ref, s32[512,128]{1,0:T(8,128)S(1)} %pad.4.row_ref, s32[4,2048]{1,0:T(4,128)S(1)} %get-tuple-element.5.lane_ref, f32[512,8,128]{2,1,0:T(8,128)S(1)} %bitcast.17, ...), custom_call_target="tpu_custom_call" | custom-call | tf_op jit(solution)/shard_map/contact/pallas_call | solution.py:522
  176.8 58.5 %scatter.1 = f32[3,49152]{1,0:T(4,128)} custom-call(s32[512,128]{1,0:T(8,128)S(1)} %bitcast.20, f32[512,4,128]{2,1,0:T(4,128)S(1)} %bitcast.18), custom_call_target="tpu_custom_call" | custom-call | tf_op jit(solution)/shard_map/scatter/pallas_call | solution.py:241
  (3 shorter events, 0.1 us)
Async XLA Ops:
  0.0 5.5 %copy-start.4 = (f32[49152]{0:T(1024)S(1)}, f32[49152]{0:T(1024)}, u32[]{:S(2)}) copy-start(f32[49152]{0:T(1024)} %param.12) | copy-start | bytes 589828
  0.0 5.6 %copy-start.3 = (f32[49152]{0:T(1024)S(1)}, f32[49152]{0:T(1024)}, u32[]{:S(2)}) copy-start(f32[49152]{0:T(1024)} %param.11) | copy-start | bytes 589828
  0.0 5.6 %copy-start.2 = (f32[3,49152]{1,0:T(4,128)S(1)}, f32[3,49152]{1,0:T(4,128)}, u32[]{:S(2)}) copy-start(f32[3,49152]{1,0:T(4,128)} %vel_ref.1) | copy-start | bytes 1769476
  0.0 5.6 %copy-start.1 = (f32[3,49152]{1,0:T(4,128)S(1)}, f32[3,49152]{1,0:T(4,128)}, u32[]{:S(2)}) copy-start(f32[3,49152]{1,0:T(4,128)} %pos_ref.1) | copy-start | bytes 1769476
  5.6 68.1 %copy-start = (s32[1024,256]{1,0:T(8,128)S(1)}, s32[1024,256]{1,0:T(8,128)}, u32[]{:S(2)}) copy-start(s32[1024,256]{1,0:T(8,128)} %mask_ref.1) | copy-start | bytes 3145732
  5.6 68.1 %copy-start.5 = (s32[2,1024]{1,0:T(2,128)S(1)}, s32[2,1024]{1,0:T(2,128)}, u32[]{:S(2)}) copy-start(s32[2,1024]{1,0:T(2,128)} %tiles_ref.1) | copy-start | bytes 24580
